TPU v7x, 256 devices: a whole 4x4x8 slice. The times are simulated.
256 devices in a mesh: frame: 32 (over y, z), head: 8 (over x, core).
Axes of the slice: x: 4, y: 4, z: 8, core: 2. Of those that a mesh axis runs over, the one named last changes fastest.
Arguments:
- queries: bfloat16 [4096, 1024], P(None, 'head'), may hold values from -8 to 8
- keys: bfloat16 [65536, 1024], P(('frame', 'head')), may hold values from -8 to 8
- values: bfloat16 [65536, 1024], P(('frame', 'head')), may hold values from -6 to 6
Outputs:
- attended: bfloat16 [4096, 1024], P('frame', 'head')
All inputs are finite; a program needn't handle non-finite values.
Results may differ from a plain program's by a relative error of at most 0.0049.
Values may be sent and summed in bfloat16 or wider, within the bound.
No kernel may reach another device: no remote copies, remote signals or barrier semaphores. Data moves between devices by JAX's collectives and lax.ppermute only.
A program may use at most 64 MiB of HBM per device.

v0:
```python
import jax
import jax.numpy as jnp
from jax import lax
from jax.sharding import PartitionSpec as P

HEAD_DIM = 64


def widen(factor):
    return jnp.repeat(factor, HEAD_DIM, axis=1)


def local(queries, keys, values):
    frames = lax.axis_size("frame")
    key_rows, value_rows = (
        lax.all_to_all(keys, "head", split_axis=1, concat_axis=0, tiled=True),
        lax.all_to_all(values, "head", split_axis=1, concat_axis=0, tiled=True),
    )
    rows = key_rows.shape[0]
    width = key_rows.shape[1]
    heads_here = width // HEAD_DIM
    count = queries.shape[0]
    scale = HEAD_DIM ** (-0.5)
    block = min(256, rows)
    turns = rows // block
    key_blocks = key_rows.reshape(turns, block, heads_here, HEAD_DIM)
    value_blocks = value_rows.reshape(turns, block, heads_here, HEAD_DIM)
    query_heads = queries.reshape(count, heads_here, HEAD_DIM)

    def block_scores(key_block):
        return (
            jnp.einsum("qhd,khd->qhk", query_heads, key_block, preferred_element_type=jnp.float32)
            * scale
        )

    def find_top(best, key_block):
        return (jnp.maximum(best, jnp.max(block_scores(key_block), axis=2)), None)

    local_top, unused = lax.scan(
        find_top, jnp.full((count, heads_here), -1e30, jnp.float32), key_blocks
    )
    top = lax.pmax(local_top, "frame")

    def visit(carry, pair):
        total, gathered = carry
        key_block, value_block = pair
        weights = jnp.exp(block_scores(key_block) - top[:, :, None])
        total = total + jnp.sum(weights, axis=2)
        gathered = gathered + jnp.einsum(
            "qhk,khd->qhd",
            weights.astype(jnp.bfloat16),
            value_block,
            preferred_element_type=jnp.float32,
        )
        return ((total, gathered), None)

    start_state = (
        jnp.zeros((count, heads_here), jnp.float32),
        jnp.zeros((count, heads_here, HEAD_DIM), jnp.float32),
    )
    (total, gathered), unused = lax.scan(visit, start_state, (key_blocks, value_blocks))
    gathered = gathered.reshape(count, width)
    mine = count // frames
    summed_all, mixed_all = lax.psum((total, gathered), "frame")
    begin = lax.axis_index("frame") * mine
    summed = lax.dynamic_slice_in_dim(summed_all, begin, mine, 0)
    mixed = lax.dynamic_slice_in_dim(mixed_all, begin, mine, 0)
    return (mixed / widen(summed)).astype(jnp.bfloat16)


def solution(mesh):
    placed = (P(None, "head"), P(("frame", "head"), None), P(("frame", "head"), None))
    return jax.shard_map(
        local, mesh=mesh, in_specs=placed, out_specs=P("frame", "head"), check_vma=False
    )
```

profile of v0, /device:TPU:6, one launch (start us, length us, event | category | flops | bytes accessed | tf_op | source)
XLA Modules:
  0.0 440.6 jit_solution(12687477950249327064)
XLA Ops:
  8.6 6.3 %all-to-all-start = ((bf16[256,8,128]{0,2,1:T(8,128)(2,1)}), bf16[256,8,128]{0,2,1:T(8,128)(2,1)}, u32[]{:S(2)}, u32[]{:S(2)}) async-start(bf16[256,8,128]{0,2,1:T(8,128)(2,1)} %bitcast), calls=%async_computation | async-start | bytes 1048576 | tf_op jit(solution)/shard_map/all_to_all | solution.py:16
  18.4 4.8 %all-to-all-done = bf16[256,8,128]{0,2,1:T(8,128)(2,1)} async-done(((bf16[256,8,128]{0,2,1:T(8,128)(2,1)}), bf16[256,8,128]{0,2,1:T(8,128)(2,1)}, u32[]{:S(2)}, u32[]{:S(2)}) %all-to-all-start) | async-done | bytes 524320 | tf_op jit(solution)/shard_map/all_to_all | solution.py:16
  23.2 6.1 %all-to-all-start.1 = ((bf16[256,8,128]{0,2,1:T(8,128)(2,1)}), bf16[256,8,128]{0,2,1:T(8,128)(2,1)}, u32[]{:S(2)}, u32[]{:S(2)}) async-start(bf16[256,8,128]{0,2,1:T(8,128)(2,1)} %bitcast.62), calls=%async_computation.1 | async-start | bytes 1048576 | tf_op jit(solution)/shard_map/all_to_all | solution.py:17
  29.4 17.7 %while.24 = (s32[]{:T(128)}, f32[4096,2]{0,1:T(2,128)S(1)}, bf16[8,256,2,64]{1,3,2,0:T(8,128)(2,1)}, bf16[4096,2,64]{0,2,1:T(8,128)(2,1)S(1)}, s32[]{:T(128)}, /*index=5*/s32[]{:T(128)}) while((s32[]{:T(128)}, f32[4096,2]{0,1:T(2,128)S(1)}, bf16[8,256,2,64]{1,3,2,0:T(8,128)(2,1)}, bf16[4096,2,64]{0,2,1:T(8,128)(2,1)S(1)}, ...), condition=%wide.region_2.3_spmd.clone, body=%wide.region_0.2_spmd.clone.sunk | while | flops 272637952 | bytes 1245275 | solution.py:39
  29.4 2.1 multiply_reduce_fusion.2
  31.6 2.1 multiply_reduce_fusion.2
  33.8 2.1 multiply_reduce_fusion.2
  36.0 2.1 multiply_reduce_fusion.2
  38.2 2.1 multiply_reduce_fusion.2
  40.4 2.1 multiply_reduce_fusion.2
  42.6 2.1 multiply_reduce_fusion.2
  44.9 2.1 multiply_reduce_fusion.2
  47.1 144.5 %pmax.7 = f32[4096,2]{0,1:T(2,128)S(1)} all-reduce(f32[4096,2]{0,1:T(2,128)S(1)} %get-tuple-element.65), channel_id=1, replica_groups=mesh['frame'=32,'head'=8] {'frame'}, use_global_device_ids=true, to_apply=%region_3.4 | all-reduce | flops 8192 | bytes 65536 | tf_op jit(solution)/shard_map/pmax | solution.py:42
  191.5 91.0 %while.25 = (s32[]{:T(128)}, f32[4096,2]{0,1:T(2,128)S(1)}, f32[4096,2,64]{0,2,1:T(8,128)S(1)}, bf16[8,256,2,64]{1,3,2,0:T(8,128)(2,1)}, bf16[4096,2,64]{0,2,1:T...) while((s32[]{:T(128)}, f32[4096,2]{0,1:T(2,128)S(1)}, ...), condition=%wide.region_6.7_spmd.clone, body=%wide.region_4.6_spmd.clone.sunk | while | flops 550510592 | bytes 22347896 | solution.py:61
  191.5 6.0 %fusion.33 = (f32[4096,2]{0,1:T(2,128)S(1)}, f32[2,256,4096]{2,1,0:T(8,128)}) fusion(f32[4096,2]{0,1:T(2,128)S(1)} %get-tuple-element.244, bf16[4096,2,64]{0,2,1:T(8,128)(2,1)S(1)} %get-tuple-element.243, bf16[8,256,2,64]{1,3,2,0:T(8,128)(2,1)} %get-tuple-element.242, s32[]{:T(128)S(6)} %copy.27), kind=kOutput, calls=%fused_computation.8.clone.1 | convolution fusion | flops 274718720 | bytes 9568260 | tf_op jit(solution)/shard_map/while/body/eval_jaxpr/qhd,khd->qhk/dot_general | solution.py:32
  197.6 5.3 %fusion.34 = f32[4096,2,64]{0,2,1:T(8,128)S(1)} fusion(f32[2,256,4096]{2,1,0:T(8,128)} %get-tuple-element.202, f32[4096,2]{0,1:T(2,128)S(1)} %get-tuple-element.244, f32[4096,2,64]{0,2,1:T(8,128)S(1)} %get-tuple-element.232, pred[]{:T(512)S(6)} %compare.7, bf16[8,256,2,64]{1,3,2,0:T(8,128)(2,1)} %get-tuple-element.245, s32[]{:T(128)S(6)} %copy.27), kind=kOutput, calls=%fused_computation.10.clone.1 | convolution fusion | flops 275775488 | bytes 12681221 | tf_op jit(solution)/shard_map/while/body/eval_jaxpr/qhk,khd->qhd/dot_general | solution.py:49
  202.9 6.0 %fusion.33 = (f32[4096,2]{0,1:T(2,128)S(1)}, f32[2,256,4096]{2,1,0:T(8,128)}) fusion(f32[4096,2]{0,1:T(2,128)S(1)} %get-tuple-element.244, bf16[4096,2,64]{0,2,1:T(8,128)(2,1)S(1)} %get-tuple-element.243, bf16[8,256,2,64]{1,3,2,0:T(8,128)(2,1)} %get-tuple-element.242, s32[]{:T(128)S(6)} %copy.27), kind=kOutput, calls=%fused_computation.8.clone.1 | convolution fusion | flops 274718720 | bytes 9568260 | tf_op jit(solution)/shard_map/while/body/eval_jaxpr/qhd,khd->qhk/dot_general | solution.py:32
  208.9 5.3 %fusion.34 = f32[4096,2,64]{0,2,1:T(8,128)S(1)} fusion(f32[2,256,4096]{2,1,0:T(8,128)} %get-tuple-element.202, f32[4096,2]{0,1:T(2,128)S(1)} %get-tuple-element.244, f32[4096,2,64]{0,2,1:T(8,128)S(1)} %get-tuple-element.232, pred[]{:T(512)S(6)} %compare.7, bf16[8,256,2,64]{1,3,2,0:T(8,128)(2,1)} %get-tuple-element.245, s32[]{:T(128)S(6)} %copy.27), kind=kOutput, calls=%fused_computation.10.clone.1 | convolution fusion | flops 275775488 | bytes 12681221 | tf_op jit(solution)/shard_map/while/body/eval_jaxpr/qhk,khd->qhd/dot_general | solution.py:49
  214.3 6.0 %fusion.33 = (f32[4096,2]{0,1:T(2,128)S(1)}, f32[2,256,4096]{2,1,0:T(8,128)}) fusion(f32[4096,2]{0,1:T(2,128)S(1)} %get-tuple-element.244, bf16[4096,2,64]{0,2,1:T(8,128)(2,1)S(1)} %get-tuple-element.243, bf16[8,256,2,64]{1,3,2,0:T(8,128)(2,1)} %get-tuple-element.242, s32[]{:T(128)S(6)} %copy.27), kind=kOutput, calls=%fused_computation.8.clone.1 | convolution fusion | flops 274718720 | bytes 9568260 | tf_op jit(solution)/shard_map/while/body/eval_jaxpr/qhd,khd->qhk/dot_general | solution.py:32
  220.3 5.3 %fusion.34 = f32[4096,2,64]{0,2,1:T(8,128)S(1)} fusion(f32[2,256,4096]{2,1,0:T(8,128)} %get-tuple-element.202, f32[4096,2]{0,1:T(2,128)S(1)} %get-tuple-element.244, f32[4096,2,64]{0,2,1:T(8,128)S(1)} %get-tuple-element.232, pred[]{:T(512)S(6)} %compare.7, bf16[8,256,2,64]{1,3,2,0:T(8,128)(2,1)} %get-tuple-element.245, s32[]{:T(128)S(6)} %copy.27), kind=kOutput, calls=%fused_computation.10.clone.1 | convolution fusion | flops 275775488 | bytes 12681221 | tf_op jit(solution)/shard_map/while/body/eval_jaxpr/qhk,khd->qhd/dot_general | solution.py:49
  225.7 6.0 %fusion.33 = (f32[4096,2]{0,1:T(2,128)S(1)}, f32[2,256,4096]{2,1,0:T(8,128)}) fusion(f32[4096,2]{0,1:T(2,128)S(1)} %get-tuple-element.244, bf16[4096,2,64]{0,2,1:T(8,128)(2,1)S(1)} %get-tuple-element.243, bf16[8,256,2,64]{1,3,2,0:T(8,128)(2,1)} %get-tuple-element.242, s32[]{:T(128)S(6)} %copy.27), kind=kOutput, calls=%fused_computation.8.clone.1 | convolution fusion | flops 274718720 | bytes 9568260 | tf_op jit(solution)/shard_map/while/body/eval_jaxpr/qhd,khd->qhk/dot_general | solution.py:32
  231.7 5.3 %fusion.34 = f32[4096,2,64]{0,2,1:T(8,128)S(1)} fusion(f32[2,256,4096]{2,1,0:T(8,128)} %get-tuple-element.202, f32[4096,2]{0,1:T(2,128)S(1)} %get-tuple-element.244, f32[4096,2,64]{0,2,1:T(8,128)S(1)} %get-tuple-element.232, pred[]{:T(512)S(6)} %compare.7, bf16[8,256,2,64]{1,3,2,0:T(8,128)(2,1)} %get-tuple-element.245, s32[]{:T(128)S(6)} %copy.27), kind=kOutput, calls=%fused_computation.10.clone.1 | convolution fusion | flops 275775488 | bytes 12681221 | tf_op jit(solution)/shard_map/while/body/eval_jaxpr/qhk,khd->qhd/dot_general | solution.py:49
  237.1 6.0 %fusion.33 = (f32[4096,2]{0,1:T(2,128)S(1)}, f32[2,256,4096]{2,1,0:T(8,128)}) fusion(f32[4096,2]{0,1:T(2,128)S(1)} %get-tuple-element.244, bf16[4096,2,64]{0,2,1:T(8,128)(2,1)S(1)} %get-tuple-element.243, bf16[8,256,2,64]{1,3,2,0:T(8,128)(2,1)} %get-tuple-element.242, s32[]{:T(128)S(6)} %copy.27), kind=kOutput, calls=%fused_computation.8.clone.1 | convolution fusion | flops 274718720 | bytes 9568260 | tf_op jit(solution)/shard_map/while/body/eval_jaxpr/qhd,khd->qhk/dot_general | solution.py:32
  243.1 5.3 %fusion.34 = f32[4096,2,64]{0,2,1:T(8,128)S(1)} fusion(f32[2,256,4096]{2,1,0:T(8,128)} %get-tuple-element.202, f32[4096,2]{0,1:T(2,128)S(1)} %get-tuple-element.244, f32[4096,2,64]{0,2,1:T(8,128)S(1)} %get-tuple-element.232, pred[]{:T(512)S(6)} %compare.7, bf16[8,256,2,64]{1,3,2,0:T(8,128)(2,1)} %get-tuple-element.245, s32[]{:T(128)S(6)} %copy.27), kind=kOutput, calls=%fused_computation.10.clone.1 | convolution fusion | flops 275775488 | bytes 12681221 | tf_op jit(solution)/shard_map/while/body/eval_jaxpr/qhk,khd->qhd/dot_general | solution.py:49
  248.4 6.0 %fusion.33 = (f32[4096,2]{0,1:T(2,128)S(1)}, f32[2,256,4096]{2,1,0:T(8,128)}) fusion(f32[4096,2]{0,1:T(2,128)S(1)} %get-tuple-element.244, bf16[4096,2,64]{0,2,1:T(8,128)(2,1)S(1)} %get-tuple-element.243, bf16[8,256,2,64]{1,3,2,0:T(8,128)(2,1)} %get-tuple-element.242, s32[]{:T(128)S(6)} %copy.27), kind=kOutput, calls=%fused_computation.8.clone.1 | convolution fusion | flops 274718720 | bytes 9568260 | tf_op jit(solution)/shard_map/while/body/eval_jaxpr/qhd,khd->qhk/dot_general | solution.py:32
  254.4 5.3 %fusion.34 = f32[4096,2,64]{0,2,1:T(8,128)S(1)} fusion(f32[2,256,4096]{2,1,0:T(8,128)} %get-tuple-element.202, f32[4096,2]{0,1:T(2,128)S(1)} %get-tuple-element.244, f32[4096,2,64]{0,2,1:T(8,128)S(1)} %get-tuple-element.232, pred[]{:T(512)S(6)} %compare.7, bf16[8,256,2,64]{1,3,2,0:T(8,128)(2,1)} %get-tuple-element.245, s32[]{:T(128)S(6)} %copy.27), kind=kOutput, calls=%fused_computation.10.clone.1 | convolution fusion | flops 275775488 | bytes 12681221 | tf_op jit(solution)/shard_map/while/body/eval_jaxpr/qhk,khd->qhd/dot_general | solution.py:49
  259.8 6.0 %fusion.33 = (f32[4096,2]{0,1:T(2,128)S(1)}, f32[2,256,4096]{2,1,0:T(8,128)}) fusion(f32[4096,2]{0,1:T(2,128)S(1)} %get-tuple-element.244, bf16[4096,2,64]{0,2,1:T(8,128)(2,1)S(1)} %get-tuple-element.243, bf16[8,256,2,64]{1,3,2,0:T(8,128)(2,1)} %get-tuple-element.242, s32[]{:T(128)S(6)} %copy.27), kind=kOutput, calls=%fused_computation.8.clone.1 | convolution fusion | flops 274718720 | bytes 9568260 | tf_op jit(solution)/shard_map/while/body/eval_jaxpr/qhd,khd->qhk/dot_general | solution.py:32
  265.8 5.3 %fusion.34 = f32[4096,2,64]{0,2,1:T(8,128)S(1)} fusion(f32[2,256,4096]{2,1,0:T(8,128)} %get-tuple-element.202, f32[4096,2]{0,1:T(2,128)S(1)} %get-tuple-element.244, f32[4096,2,64]{0,2,1:T(8,128)S(1)} %get-tuple-element.232, pred[]{:T(512)S(6)} %compare.7, bf16[8,256,2,64]{1,3,2,0:T(8,128)(2,1)} %get-tuple-element.245, s32[]{:T(128)S(6)} %copy.27), kind=kOutput, calls=%fused_computation.10.clone.1 | convolution fusion | flops 275775488 | bytes 12681221 | tf_op jit(solution)/shard_map/while/body/eval_jaxpr/qhk,khd->qhd/dot_general | solution.py:49
  271.2 6.0 %fusion.33 = (f32[4096,2]{0,1:T(2,128)S(1)}, f32[2,256,4096]{2,1,0:T(8,128)}) fusion(f32[4096,2]{0,1:T(2,128)S(1)} %get-tuple-element.244, bf16[4096,2,64]{0,2,1:T(8,128)(2,1)S(1)} %get-tuple-element.243, bf16[8,256,2,64]{1,3,2,0:T(8,128)(2,1)} %get-tuple-element.242, s32[]{:T(128)S(6)} %copy.27), kind=kOutput, calls=%fused_computation.8.clone.1 | convolution fusion | flops 274718720 | bytes 9568260 | tf_op jit(solution)/shard_map/while/body/eval_jaxpr/qhd,khd->qhk/dot_general | solution.py:32
  277.2 5.3 %fusion.34 = f32[4096,2,64]{0,2,1:T(8,128)S(1)} fusion(f32[2,256,4096]{2,1,0:T(8,128)} %get-tuple-element.202, f32[4096,2]{0,1:T(2,128)S(1)} %get-tuple-element.244, f32[4096,2,64]{0,2,1:T(8,128)S(1)} %get-tuple-element.232, pred[]{:T(512)S(6)} %compare.7, bf16[8,256,2,64]{1,3,2,0:T(8,128)(2,1)} %get-tuple-element.245, s32[]{:T(128)S(6)} %copy.27), kind=kOutput, calls=%fused_computation.10.clone.1 | convolution fusion | flops 275775488 | bytes 12681221 | tf_op jit(solution)/shard_map/while/body/eval_jaxpr/qhk,khd->qhd/dot_general | solution.py:49
  283.9 138.1 %psum.15 = f32[4096,2]{0,1:T(2,128)S(1)} all-reduce(f32[4096,2]{0,1:T(2,128)S(1)} %get-tuple-element.67), channel_id=1, replica_groups=mesh['frame'=32,'head'=8] {'frame'}, use_global_device_ids=true, to_apply=%region_8.9 | all-reduce | flops 8192 | bytes 65536 | tf_op jit(solution)/shard_map/psum | solution.py:64
  422.0 10.2 %all-reduce.2.cloned.1.call-done = f32[4096,128]{0,1:T(8,128)} async-done(((f32[4096,128]{0,1:T(8,128)}), f32[4096,128]{0,1:T(8,128)}) %all-reduce.2.cloned.1.call-update) | async-done | bytes 2097168 | tf_op jit(solution)/shard_map/psum | solution.py:64
  (30 shorter events, 9.1 us)
Async XLA Ops:
  8.6 14.6 %all-to-all-start = ((bf16[256,8,128]{0,2,1:T(8,128)(2,1)}), bf16[256,8,128]{0,2,1:T(8,128)(2,1)}, u32[]{:S(2)}, u32[]{:S(2)}) async-start(bf16[256,8,128]{0,2,1:T(8,128)(2,1)} %bitcast), calls=%async_computation | async-start | bytes 1048576 | tf_op jit(solution)/shard_map/all_to_all | solution.py:16
  23.2 168.3 %all-to-all-start.1 = ((bf16[256,8,128]{0,2,1:T(8,128)(2,1)}), bf16[256,8,128]{0,2,1:T(8,128)(2,1)}, u32[]{:S(2)}, u32[]{:S(2)}) async-start(bf16[256,8,128]{0,2,1:T(8,128)(2,1)} %bitcast.62), calls=%async_computation.1 | async-start | bytes 1048576 | tf_op jit(solution)/shard_map/all_to_all | solution.py:17
  29.4 402.8 %all-reduce.2.cloned.1.call-start = ((), (), s32[]{:S(2)}) async-start(), calls=%async_computation.2 | async-start | bytes 4194304 | tf_op jit(solution)/shard_map/psum | solution.py:64
  282.6 1.3 copy-start
Sparse Core Ops, SparseCore 0:
  284.0 148.1 all-reduce.1
where the time goes:
time: 442 us; the launch traced here: 441 us
  blocking collectives  283 us (64%)
  matrix products  108 us (24%)
  waiting for transfers between devices  15.1 us (3%)
  between operations  13.4 us (3%)
  starting transfers between devices  12.4 us (3%)
  local copies, waits for them, and re-layouts  7.59 us (2%)
    pmax x1, blocking collectives, local(): top = lax.pmax(local_top, 'frame')  144 us
    psum x1, blocking collectives, local(): summed_all, mixed_all = lax.psum((total, gathered), 'frame')  138 us
    dot_general x16, matrix products, block_scores(): jnp.einsum('qhd,khd->qhk', query_heads, key_block, preferred_element_type...  64.8 us
    dot_general x8, matrix products, visit(): jnp.einsum('qhk,khd->qhd', weights.astype(jnp.bfloat16), value_block, pre...  42.8 us
    psum x1, waiting for transfers between devices, local(): summed_all, mixed_all = lax.psum((total, gathered), 'frame')  10.2 us
  transfers between devices with their start and end apart: 3, of which 2 were waited for; matrix products, arithmetic and copies ran while one was open for 5% of the time, Pallas kernels for 0%

commit v1 on v0

v1 whole, which is shorter than its diff:
```python
import functools

import jax
import jax.numpy as jnp
from jax import lax
from jax.experimental import pallas as pl
from jax.experimental.pallas import tpu as pltpu
from jax.sharding import PartitionSpec as P

HEAD_DIM = 64
HEADS_HERE = 2
RIM = 16
ROWS = HEAD_DIM + RIM
SCALE = 1.4426950408889634 * HEAD_DIM ** (-0.5)
Y = 4
Z = 8
TILE = 512
BF = jnp.bfloat16
F32 = jnp.float32
VMEM = pl.BlockSpec(memory_space=pltpu.VMEM)


def call(body, inputs, outs, name, scratch=(), flops=0, exps=0):
    return pl.pallas_call(
        body,
        out_shape=outs,
        in_specs=[VMEM] * len(inputs),
        out_specs=jax.tree.map(lambda _: VMEM, outs),
        scratch_shapes=list(scratch),
        name=name,
        compiler_params=pltpu.CompilerParams(vmem_limit_bytes=40 << 20),
        cost_estimate=pl.CostEstimate(flops=flops, transcendentals=exps, bytes_accessed=1 << 20),
    )(*inputs)


def pack_body(keys, values, first, second):
    for j in range(first.shape[0]):
        k = keys[:, 128 * j : 128 * j + 128]
        v = values[:, 128 * j : 128 * j + 128]
        first[j] = jnp.concatenate([k[:, :HEAD_DIM], v[:, :HEAD_DIM]], axis=1)
        second[j] = jnp.concatenate([k[:, HEAD_DIM:], v[:, HEAD_DIM:]], axis=1)


def turn_body(queries, first, second):
    count = queries.shape[0]
    for i in range(0, count, TILE):
        t = queries[i : i + TILE, :].T
        none = jnp.zeros((HEAD_DIM, TILE), BF)
        first[:HEAD_DIM, i : i + TILE] = t[:HEAD_DIM]
        first[HEAD_DIM:, i : i + TILE] = none
        second[:HEAD_DIM, i : i + TILE] = t[HEAD_DIM:]
        second[HEAD_DIM:, i : i + TILE] = none


def prep_body(pairs, out):
    t = pairs[...].T
    out[:HEAD_DIM] = t[HEAD_DIM:]
    out[HEAD_DIM:] = jnp.ones((RIM, t.shape[1]), BF)


def write_rim(lse):
    high = lse.astype(BF).astype(F32)
    rest = lse - high
    mid = rest.astype(BF).astype(F32)
    low = rest - mid
    row = lax.broadcasted_iota(jnp.int32, (RIM, lse.shape[1]), 0)
    return jnp.where(row == 0, high, jnp.where(row == 1, mid, jnp.where(row == 2, low, 0.0)))


def attend_body(shifts, queries, pairs, turned, *rest):
    outs, (even, odd) = rest[: len(shifts)], rest[len(shifts) :]
    block = outs[0].shape[1]
    y = lax.axis_index("frame") // Z
    tiles = [(b, i) for b in range(len(shifts)) for i in range(block // TILE)]

    def score(t, held):
        b, i = tiles[t]
        start = pl.multiple_of(lax.rem(y + shifts[b], Y) * block + i * TILE, TILE)
        held[...] = jnp.dot(
            pairs[...], queries[:, pl.ds(start, TILE)], preferred_element_type=F32
        )

    def gather(t, held):
        b, i = tiles[t]
        top = jnp.max(held[...], axis=0, keepdims=True) * SCALE
        weights = jnp.exp2(held[...] * SCALE - top).astype(BF)
        mixed = jnp.dot(turned[...], weights, preferred_element_type=F32)
        total = mixed[HEAD_DIM : HEAD_DIM + 1]
        span = slice(i * TILE, i * TILE + TILE)
        outs[b][:HEAD_DIM, span] = (mixed[:HEAD_DIM] / total).astype(BF)
        outs[b][HEAD_DIM:, span] = write_rim(top + jnp.log2(total)).astype(BF)

    score(0, even)
    for t in range(len(tiles)):
        here, there = (even, odd) if t % 2 == 0 else (odd, even)
        if t + 1 < len(tiles):
            score(t + 1, there)
        gather(t, here)


def attend(shifts, queries, pairs, turned, block):
    rows = pairs.shape[0]
    outs = [jax.ShapeDtypeStruct((ROWS, block), BF) for _ in shifts]
    work = len(shifts) * block * rows
    return call(
        functools.partial(attend_body, shifts),
        (queries, pairs, turned),
        outs,
        "attend",
        scratch=[pltpu.VMEM((rows, TILE), F32)] * 2,
        flops=work * 512,
        exps=work,
    )


def merge(parts):
    logs = [jnp.sum(p[HEAD_DIM:].astype(F32), axis=0, keepdims=True) for p in parts]
    top = functools.reduce(jnp.maximum, logs)
    shares = [jnp.exp2(l - top) for l in logs]
    total = functools.reduce(jnp.add, shares)
    mixed = functools.reduce(
        jnp.add, [p[:HEAD_DIM].astype(F32) * s for p, s in zip(parts, shares)]
    )
    return mixed / total, top + jnp.log2(total)


def merge_body(cuts, position, parts, *refs):
    ins, outs = refs[:parts], refs[parts:]
    width = outs[0].shape[1]
    me = position()
    for k, out in enumerate(outs):
        start = pl.multiple_of(lax.rem(me + k, cuts) * width, width)
        mixed, lse = merge([r[:, pl.ds(start, width)] for r in ins])
        out[:HEAD_DIM] = mixed.astype(BF)
        out[HEAD_DIM:] = write_rim(lse).astype(BF)


def split_merge(parts, cuts, position):
    width = parts[0].shape[1] // cuts
    outs = [jax.ShapeDtypeStruct((ROWS, width), BF) for _ in range(cuts)]
    return call(
        functools.partial(merge_body, cuts, position, len(parts)), parts, outs, "merge"
    )


def last_body(first_a, first_b, second_a, second_b, out):
    first, unused = merge([first_a[...], first_b[...]])
    second, unused = merge([second_a[...], second_b[...]])
    out[...] = jnp.concatenate([first, second], axis=0).T.astype(BF)


def move(x, target):
    return lax.ppermute(x, "frame", [(f, target(f // Z, f % Z)) for f in range(Y * Z)])


def half_of_z():
    return lax.rem(lax.axis_index("frame"), Z) // 2


def odd_of_z():
    return lax.rem(lax.axis_index("frame"), 2)


def local(queries, keys, values):
    count = queries.shape[0]
    block = count // Y
    ranks = lax.axis_size("head")
    tokens = keys.shape[0]
    sent = call(
        pack_body,
        (keys, values),
        [jax.ShapeDtypeStruct((ranks, tokens, 128), BF)] * HEADS_HERE,
        "pack",
    )
    arrived = [lax.all_to_all(x, "head", 0, 0, tiled=True) for x in sent]
    turned_queries = call(
        turn_body, (queries,), [jax.ShapeDtypeStruct((128, count), BF)] * HEADS_HERE, "turn"
    )
    ends = []
    for head in range(HEADS_HERE):
        pairs = arrived[head].reshape(ranks * tokens, 128)
        turned = call(
            prep_body, (pairs,), jax.ShapeDtypeStruct((ROWS, ranks * tokens), BF), "prep"
        )
        parts = []
        for shift in (2, 1, 3, 0):
            (part,) = attend((shift,), turned_queries[head], pairs, turned, block)
            if shift:
                part = move(part, lambda y, z: (y + shift) % Y * Z + z)
            parts.append(part)
        pieces = split_merge(parts, Z // 2, half_of_z)
        parts = [pieces[0]]
        for k in range(1, Z // 2):
            parts.append(move(pieces[k], lambda y, z: y * Z + (z + 2 * k) % Z))
        mine, other = split_merge(parts, 2, odd_of_z)
        ends += [mine, move(other, lambda y, z: y * Z + (z ^ 1))]
    return call(last_body, ends, jax.ShapeDtypeStruct((count // Y // Z, 128), BF), "last")


def solution(mesh):
    placed = (P(None, "head"), P(("frame", "head"), None), P(("frame", "head"), None))
    return jax.shard_map(
        local, mesh=mesh, in_specs=placed, out_specs=P("frame", "head"), check_vma=False
    )
```

time: 442 us -> 84.1 us (0.19)
  blocking collectives: 283 us -> 13.1 us
  matrix products: 108 us -> 0 us
  Pallas kernels: 0 us -> 28.1 us
  starting transfers between devices: 12.4 us -> 32.9 us
  between operations: 13.4 us -> 0.17 us
  waiting for transfers between devices: 15.1 us -> 6.95 us
  local copies, waits for them, and re-layouts: 7.59 us -> 2.09 us
    pmax x1 -> x0, blocking collectives: 144 us -> none  [local(): top = lax.pmax(local_top, 'frame')]
    psum x1 -> x0, blocking collectives: 138 us -> none  [local(): summed_all, mixed_all = lax.psum((total, gathered), 'frame')]
    dot_general x24 -> x0, matrix products: 108 us -> none  [the longest x16 64.8 us: block_scores(): jnp.einsum('qhd,khd->qhk', query_heads, key_block, preferred_element_type...]
    pallas_call x0 -> x17, Pallas kernels: none -> 28.1 us  [call(): pl.pallas_call(body, out_shape=outs, in_specs=[VMEM] * len(inputs), out_s...]
    ppermute x0 -> x14, starting transfers between devices: none -> 27.4 us  [move(): lax.ppermute(x, 'frame', [(f, target(f // Z, f % Z)) for f in range(Y * Z)])]
    all_to_all x0 -> x1, blocking collectives: none -> 13.1 us  [local(): arrived = [lax.all_to_all(x, 'head', 0, 0, tiled=True) for x in sent]]
    psum x1 -> x0, waiting for transfers between devices: 10.2 us -> none  [local(): summed_all, mixed_all = lax.psum((total, gathered), 'frame')]
    ppermute x0 -> x14, waiting for transfers between devices: none -> 6.95 us  [move(): lax.ppermute(x, 'frame', [(f, target(f // Z, f % Z)) for f in range(Y * Z)])]
  transfers between devices with their start and end apart: 3 -> 15, of which waited for: 2 -> 4; matrix products, arithmetic and copies ran while one was open for 5% -> 0% of each run, Pallas kernels for 0% -> 31%
where the time goes in v1:
time: 84.1 us; the launch traced here: 83.2 us
  starting transfers between devices  32.9 us (39%)
  Pallas kernels  28.1 us (33%)
  blocking collectives  13.1 us (16%)
  waiting for transfers between devices  6.95 us (8%)
  local copies, waits for them, and re-layouts  2.09 us (2%)
    pallas_call x17, Pallas kernels, call(): pl.pallas_call(body, out_shape=outs, in_specs=[VMEM] * len(inputs), out_s...  28.1 us
    ppermute x14, starting transfers between devices, move(): lax.ppermute(x, 'frame', [(f, target(f // Z, f % Z)) for f in range(Y * Z)])  27.4 us
    all_to_all x1, blocking collectives, local(): arrived = [lax.all_to_all(x, 'head', 0, 0, tiled=True) for x in sent]  13.1 us
    ppermute x14, waiting for transfers between devices, move(): lax.ppermute(x, 'frame', [(f, target(f // Z, f % Z)) for f in range(Y * Z)])  6.95 us
    all_to_all x1, starting transfers between devices, local(): arrived = [lax.all_to_all(x, 'head', 0, 0, tiled=True) for x in sent]  5.5 us
    unnamed x10, local copies, waits for them, and re-layouts  2.09 us
  transfers between devices with their start and end apart: 15, of which 4 were waited for; matrix products, arithmetic and copies ran while one was open for 0% of the time, Pallas kernels for 31%

profile of v1, /device:TPU:6, one launch (start us, length us, event | category | flops | bytes accessed | tf_op | source)
XLA Modules:
  0.0 83.2 jit_solution(1999963465628224019)
XLA Ops:
  0.0 1.0 %copy-done.1 = bf16[256,1024]{1,0:T(8,128)(2,1)S(1)} copy-done((bf16[256,1024]{1,0:T(8,128)(2,1)S(1)}, bf16[256,1024]{1,0:T(8,128)(2,1)}, u32[]{:S(2)}) %copy-start.1) | copy-done | bytes 524312
  1.0 1.0 %copy-done.2 = bf16[256,1024]{1,0:T(8,128)(2,1)S(1)} copy-done((bf16[256,1024]{1,0:T(8,128)(2,1)S(1)}, bf16[256,1024]{1,0:T(8,128)(2,1)}, u32[]{:S(2)}) %copy-start.2) | copy-done | bytes 524312
  2.1 1.1 %pack.1 = (bf16[8,256,128]{2,1,0:T(8,128)(2,1)}, bf16[8,256,128]{2,1,0:T(8,128)(2,1)S(1)}) custom-call(bf16[256,1024]{1,0:T(8,128)(2,1)S(1)} %copy-done.1, bf16[256,1024]{1,0:T(8,128)(2,1)S(1)} %copy-done.2), custom_call_target="tpu_custom_call" | custom-call | bytes 1048576 | tf_op jit(solution)/shard_map/pack/pallas_call | solution.py:24
  3.2 13.1 %all_to_all.10 = bf16[8,256,128]{2,1,0:T(8,128)(2,1)S(1)} all-to-all(bf16[8,256,128]{2,1,0:T(8,128)(2,1)S(1)} %get-tuple-element.30), channel_id=1, replica_groups=mesh['frame'=32,'head'=8] {'head'}, dimensions={0} | all-to-all | bytes 1048576 | tf_op jit(solution)/shard_map/all_to_all | solution.py:175
  16.3 5.5 %all-to-all-start = ((bf16[8,256,128]{2,1,0:T(8,128)(2,1)}), bf16[8,256,128]{2,1,0:T(8,128)(2,1)S(1)}, u32[]{:S(2)}, u32[]{:S(2)}) async-start(bf16[8,256,128]{2,1,0:T(8,128)(2,1)} %get-tuple-element.22), calls=%async_computation | async-start | bytes 1048576 | tf_op jit(solution)/shard_map/all_to_all | solution.py:175
  21.8 0.3 turn.1
  22.3 3.7 %attend.12 = bf16[80,1024]{1,0:T(8,128)(2,1)} custom-call(bf16[128,4096]{1,0:T(8,128)(2,1)S(1)} %get-tuple-element.29.queries, bf16[2048,128]{1,0:T(8,128)(2,1)S(1)} %bitcast.8, bf16[80,2048]{1,0:T(8,128)(2,1)S(1)} %prep.3.turned), custom_call_target="tpu_custom_call" | custom-call | flops 1073741824 | bytes 1048576 | tf_op jit(solution)/shard_map/attend/pallas_call | solution.py:24
  26.1 3.2 %collective-permute-start.7 = (bf16[80,1024]{1,0:T(8,128)(2,1)}, bf16[80,1024]{1,0:T(8,128)(2,1)S(1)}, u32[]{:S(2)}, u32[]{:S(2)}) collective-permute-start(bf16[80,1024]{1,0:T(8,128)(2,1)} %attend.12), channel_id=1, source_target_pairs={{0,128},{8,136},{16,144},{24,152},{32,160},{40,168},{48,176},{56,1... | collective-permute-start | bytes 491528 | tf_op jit(solution)/shard_map/ppermute | solution.py:153
  29.2 3.0 %attend.13 = bf16[80,1024]{1,0:T(8,128)(2,1)S(1)} custom-call(bf16[128,4096]{1,0:T(8,128)(2,1)S(1)} %get-tuple-element.29.queries, bf16[2048,128]{1,0:T(8,128)(2,1)S(1)} %bitcast.9, bf16[80,2048]{1,0:T(8,128)(2,1)S(1)} %prep.3.turned), custom_call_target="tpu_custom_call" | custom-call | flops 1073741824 | bytes 1048576 | tf_op jit(solution)/shard_map/attend/pallas_call | solution.py:24
  32.2 0.8 collective-permute-start.8
  33.0 3.0 %attend.14 = bf16[80,1024]{1,0:T(8,128)(2,1)S(1)} custom-call(bf16[128,4096]{1,0:T(8,128)(2,1)S(1)} %get-tuple-element.29.queries, bf16[2048,128]{1,0:T(8,128)(2,1)S(1)} %bitcast.10, bf16[80,2048]{1,0:T(8,128)(2,1)S(1)} %prep.3.turned), custom_call_target="tpu_custom_call" | custom-call | flops 1073741824 | bytes 1048576 | tf_op jit(solution)/shard_map/attend/pallas_call | solution.py:24
  36.0 2.8 %collective-permute-start.9 = (bf16[80,1024]{1,0:T(8,128)(2,1)S(1)}, bf16[80,1024]{1,0:T(8,128)(2,1)S(1)}, u32[]{:S(2)}, u32[]{:S(2)}) collective-permute-start(bf16[80,1024]{1,0:T(8,128)(2,1)S(1)} %attend.14), channel_id=1, source_target_pairs={{0,192},{8,200},{16,208},{24,216},{32,224},{40,232},{48,240},{56,2... | collective-permute-start | bytes 491528 | tf_op jit(solution)/shard_map/ppermute | solution.py:153
  39.0 3.0 %attend.10 = bf16[80,1024]{1,0:T(8,128)(2,1)S(1)} custom-call(bf16[128,4096]{1,0:T(8,128)(2,1)S(1)} %get-tuple-element.21.queries, bf16[2048,128]{1,0:T(8,128)(2,1)S(1)} %bitcast.3, bf16[80,2048]{1,0:T(8,128)(2,1)S(1)} %prep.2.turned), custom_call_target="tpu_custom_call" | custom-call | flops 1073741824 | bytes 1048576 | tf_op jit(solution)/shard_map/attend/pallas_call | solution.py:24
  42.2 3.0 %attend.9 = bf16[80,1024]{1,0:T(8,128)(2,1)S(1)} custom-call(bf16[128,4096]{1,0:T(8,128)(2,1)S(1)} %get-tuple-element.21.queries, bf16[2048,128]{1,0:T(8,128)(2,1)S(1)} %bitcast.4, bf16[80,2048]{1,0:T(8,128)(2,1)S(1)} %prep.2.turned), custom_call_target="tpu_custom_call" | custom-call | flops 1073741824 | bytes 1048576 | tf_op jit(solution)/shard_map/attend/pallas_call | solution.py:24
  45.2 2.1 %collective-permute-start.1 = (bf16[80,1024]{1,0:T(8,128)(2,1)S(1)}, bf16[80,1024]{1,0:T(8,128)(2,1)S(1)}, u32[]{:S(2)}, u32[]{:S(2)}) collective-permute-start(bf16[80,1024]{1,0:T(8,128)(2,1)S(1)} %attend.9), channel_id=1, source_target_pairs={{0,64},{8,72},{16,80},{24,88},{32,96},{40,104},{48,112},{56,120},{... | collective-permute-start | bytes 491528 | tf_op jit(solution)/shard_map/ppermute | solution.py:153
  47.3 3.0 %attend.8 = bf16[80,1024]{1,0:T(8,128)(2,1)S(1)} custom-call(bf16[128,4096]{1,0:T(8,128)(2,1)S(1)} %get-tuple-element.21.queries, bf16[2048,128]{1,0:T(8,128)(2,1)S(1)} %bitcast.5, bf16[80,2048]{1,0:T(8,128)(2,1)S(1)} %prep.2.turned), custom_call_target="tpu_custom_call" | custom-call | flops 1073741824 | bytes 1048576 | tf_op jit(solution)/shard_map/attend/pallas_call | solution.py:24
  50.3 0.3 collective-permute-start
  50.7 3.0 %attend.15.refs_3_ = bf16[80,1024]{1,0:T(8,128)(2,1)S(1)} custom-call(bf16[128,4096]{1,0:T(8,128)(2,1)S(1)} %copy-done.4, bf16[2048,128]{1,0:T(8,128)(2,1)S(1)} %bitcast.11, bf16[80,2048]{1,0:T(8,128)(2,1)S(1)} %prep.3.turned), custom_call_target="tpu_custom_call" | custom-call | flops 1073741824 | bytes 1048576 | tf_op jit(solution)/shard_map/attend/pallas_call | solution.py:24
  53.7 0.2 merge.6
  54.0 3.3 %collective-permute-start.10 = (bf16[80,256]{1,0:T(8,128)(2,1)S(1)}, bf16[80,256]{1,0:T(8,128)(2,1)S(1)}, u32[]{:S(2)}, u32[]{:S(2)}) collective-permute-start(bf16[80,256]{1,0:T(8,128)(2,1)S(1)} %get-tuple-element.32), channel_id=1, source_target_pairs={{0,16},{8,24},{16,32},{24,40},{32,48},{40,56},{48,0},{56,8},{64,80... | collective-permute-start | bytes 122888 | tf_op jit(solution)/shard_map/ppermute | solution.py:153
  57.3 3.0 %attend.11.refs_3_ = bf16[80,1024]{1,0:T(8,128)(2,1)S(1)} custom-call(bf16[128,4096]{1,0:T(8,128)(2,1)S(1)} %get-tuple-element.21.queries, bf16[2048,128]{1,0:T(8,128)(2,1)S(1)} %bitcast.6, bf16[80,2048]{1,0:T(8,128)(2,1)S(1)} %prep.2.turned), custom_call_target="tpu_custom_call" | custom-call | flops 1073741824 | bytes 1048576 | tf_op jit(solution)/shard_map/attend/pallas_call | solution.py:24
  60.3 5.5 %collective-permute-start.11 = (bf16[80,256]{1,0:T(8,128)(2,1)S(1)}, bf16[80,256]{1,0:T(8,128)(2,1)S(1)}, u32[]{:S(2)}, u32[]{:S(2)}) collective-permute-start(bf16[80,256]{1,0:T(8,128)(2,1)S(1)} %get-tuple-element.33), channel_id=1, source_target_pairs={{0,32},{8,40},{16,48},{24,56},{32,0},{40,8},{48,16},{56,24},{64,96... | collective-permute-start | bytes 122888 | tf_op jit(solution)/shard_map/ppermute | solution.py:153
  65.8 2.6 %collective-permute-start.12 = (bf16[80,256]{1,0:T(8,128)(2,1)S(1)}, bf16[80,256]{1,0:T(8,128)(2,1)S(1)}, u32[]{:S(2)}, u32[]{:S(2)}) collective-permute-start(bf16[80,256]{1,0:T(8,128)(2,1)S(1)} %get-tuple-element.34), channel_id=1, source_target_pairs={{0,48},{8,56},{16,0},{24,8},{32,16},{40,24},{48,32},{56,40},{64,11... | collective-permute-start | bytes 122888 | tf_op jit(solution)/shard_map/ppermute | solution.py:153
  68.7 0.4 collective-permute-start.3
  69.1 2.1 %collective-permute-start.4 = (bf16[80,256]{1,0:T(8,128)(2,1)S(1)}, bf16[80,256]{1,0:T(8,128)(2,1)S(1)}, u32[]{:S(2)}, u32[]{:S(2)}) collective-permute-start(bf16[80,256]{1,0:T(8,128)(2,1)S(1)} %get-tuple-element.25), channel_id=1, source_target_pairs={{0,32},{8,40},{16,48},{24,56},{32,0},{40,8},{48,16},{56,24},{64,96... | collective-permute-start | bytes 122888 | tf_op jit(solution)/shard_map/ppermute | solution.py:153
  71.2 2.7 %collective-permute-start.5 = (bf16[80,256]{1,0:T(8,128)(2,1)S(1)}, bf16[80,256]{1,0:T(8,128)(2,1)S(1)}, u32[]{:S(2)}, u32[]{:S(2)}) collective-permute-start(bf16[80,256]{1,0:T(8,128)(2,1)S(1)} %get-tuple-element.26), channel_id=1, source_target_pairs={{0,48},{8,56},{16,0},{24,8},{32,16},{40,24},{48,32},{56,40},{64,11... | collective-permute-start | bytes 122888 | tf_op jit(solution)/shard_map/ppermute | solution.py:153
  73.9 1.1 %collective-permute-start.13 = (bf16[80,128]{1,0:T(8,128)(2,1)S(1)}, bf16[80,128]{1,0:T(8,128)(2,1)S(1)}, u32[]{:S(2)}, u32[]{:S(2)}) collective-permute-start(bf16[80,128]{1,0:T(8,128)(2,1)S(1)} %get-tuple-element.36), channel_id=1, source_target_pairs={{0,8},{8,0},{16,24},{24,16},{32,40},{40,32},{48,56},{56,48},{64,72... | collective-permute-start | bytes 61448 | tf_op jit(solution)/shard_map/ppermute | solution.py:153
  75.1 2.3 %collective-permute-done.4.refs_2_ = bf16[80,256]{1,0:T(8,128)(2,1)S(1)} collective-permute-done((bf16[80,256]{1,0:T(8,128)(2,1)S(1)}, bf16[80,256]{1,0:T(8,128)(2,1)S(1)}, u32[]{:S(2)}, u32[]{:S(2)}) %collective-permute-start.4) | collective-permute-done | bytes 40992 | tf_op jit(solution)/shard_map/ppermute | solution.py:153
  77.4 1.2 %collective-permute-done.5.refs_3_ = bf16[80,256]{1,0:T(8,128)(2,1)S(1)} collective-permute-done((bf16[80,256]{1,0:T(8,128)(2,1)S(1)}, bf16[80,256]{1,0:T(8,128)(2,1)S(1)}, u32[]{:S(2)}, u32[]{:S(2)}) %collective-permute-start.5) | collective-permute-done | bytes 40992 | tf_op jit(solution)/shard_map/ppermute | solution.py:153
  78.6 0.5 collective-permute-start.6
  79.1 3.4 %collective-permute-done.6.first_b = bf16[80,128]{1,0:T(8,128)(2,1)S(1)} collective-permute-done((bf16[80,128]{1,0:T(8,128)(2,1)S(1)}, bf16[80,128]{1,0:T(8,128)(2,1)S(1)}, u32[]{:S(2)}, u32[]{:S(2)}) %collective-permute-start.6) | collective-permute-done | bytes 20512 | tf_op jit(solution)/shard_map/ppermute | solution.py:153
  82.5 0.7 last.1
  (26 shorter events, 0.9 us)
Async XLA Ops:
  0.0 1.0 %copy-start.1 = (bf16[256,1024]{1,0:T(8,128)(2,1)S(1)}, bf16[256,1024]{1,0:T(8,128)(2,1)}, u32[]{:S(2)}) copy-start(bf16[256,1024]{1,0:T(8,128)(2,1)} %keys.1) | copy-start | bytes 1572868
  1.0 1.0 %copy-start.2 = (bf16[256,1024]{1,0:T(8,128)(2,1)S(1)}, bf16[256,1024]{1,0:T(8,128)(2,1)}, u32[]{:S(2)}) copy-start(bf16[256,1024]{1,0:T(8,128)(2,1)} %values.1) | copy-start | bytes 1572868
  3.2 18.6 %copy-start = (bf16[4096,128]{1,0:T(8,128)(2,1)S(1)}, bf16[4096,128]{1,0:T(8,128)(2,1)}, u32[]{:S(2)}) copy-start(bf16[4096,128]{1,0:T(8,128)(2,1)} %queries.1) | copy-start | bytes 3145732
  16.3 22.5 %all-to-all-start = ((bf16[8,256,128]{2,1,0:T(8,128)(2,1)}), bf16[8,256,128]{2,1,0:T(8,128)(2,1)S(1)}, u32[]{:S(2)}, u32[]{:S(2)}) async-start(bf16[8,256,128]{2,1,0:T(8,128)(2,1)} %get-tuple-element.22), calls=%async_computation | async-start | bytes 1048576 | tf_op jit(solution)/shard_map/all_to_all | solution.py:175
  22.1 10.8 %copy-start.3 = (bf16[128,4096]{1,0:T(8,128)(2,1)}, bf16[128,4096]{1,0:T(8,128)(2,1)S(1)}, u32[]{:S(2)}) copy-start(bf16[128,4096]{1,0:T(8,128)(2,1)S(1)} %get-tuple-element.29.queries) | copy-start | bytes 3145732
  26.1 24.3 %collective-permute-start.7 = (bf16[80,1024]{1,0:T(8,128)(2,1)}, bf16[80,1024]{1,0:T(8,128)(2,1)S(1)}, u32[]{:S(2)}, u32[]{:S(2)}) collective-permute-start(bf16[80,1024]{1,0:T(8,128)(2,1)} %attend.12), channel_id=1, source_target_pairs={{0,128},{8,136},{16,144},{24,152},{32,160},{40,168},{48,176},{56,1... | collective-permute-start | bytes 491528 | tf_op jit(solution)/shard_map/ppermute | solution.py:153
  32.2 21.5 %collective-permute-start.8 = (bf16[80,1024]{1,0:T(8,128)(2,1)S(1)}, bf16[80,1024]{1,0:T(8,128)(2,1)S(1)}, u32[]{:S(2)}, u32[]{:S(2)}) collective-permute-start(bf16[80,1024]{1,0:T(8,128)(2,1)S(1)} %attend.13), channel_id=1, source_target_pairs={{0,64},{8,72},{16,80},{24,88},{32,96},{40,104},{48,112},{56,120},{... | collective-permute-start | bytes 491528 | tf_op jit(solution)/shard_map/ppermute | solution.py:153
  36.0 17.7 %collective-permute-start.9 = (bf16[80,1024]{1,0:T(8,128)(2,1)S(1)}, bf16[80,1024]{1,0:T(8,128)(2,1)S(1)}, u32[]{:S(2)}, u32[]{:S(2)}) collective-permute-start(bf16[80,1024]{1,0:T(8,128)(2,1)S(1)} %attend.14), channel_id=1, source_target_pairs={{0,192},{8,200},{16,208},{24,216},{32,224},{40,232},{48,240},{56,2... | collective-permute-start | bytes 491528 | tf_op jit(solution)/shard_map/ppermute | solution.py:153
  42.1 23.7 %collective-permute-start.2 = (bf16[80,1024]{1,0:T(8,128)(2,1)S(1)}, bf16[80,1024]{1,0:T(8,128)(2,1)S(1)}, u32[]{:S(2)}, u32[]{:S(2)}) collective-permute-start(bf16[80,1024]{1,0:T(8,128)(2,1)S(1)} %attend.10), channel_id=1, source_target_pairs={{0,192},{8,200},{16,208},{24,216},{32,224},{40,232},{48,240},{56,2... | collective-permute-start | bytes 491528 | tf_op jit(solution)/shard_map/ppermute | solution.py:153
  45.2 5.4 %copy-start.4 = (bf16[128,4096]{1,0:T(8,128)(2,1)S(1)}, bf16[128,4096]{1,0:T(8,128)(2,1)}, u32[]{:S(2)}) copy-start(bf16[128,4096]{1,0:T(8,128)(2,1)} %copy-done.3) | copy-start | bytes 3145732
  45.2 23.2 %collective-permute-start.1 = (bf16[80,1024]{1,0:T(8,128)(2,1)S(1)}, bf16[80,1024]{1,0:T(8,128)(2,1)S(1)}, u32[]{:S(2)}, u32[]{:S(2)}) collective-permute-start(bf16[80,1024]{1,0:T(8,128)(2,1)S(1)} %attend.9), channel_id=1, source_target_pairs={{0,64},{8,72},{16,80},{24,88},{32,96},{40,104},{48,112},{56,120},{... | collective-permute-start | bytes 491528 | tf_op jit(solution)/shard_map/ppermute | solution.py:153
  50.3 18.1 %collective-permute-start = (bf16[80,1024]{1,0:T(8,128)(2,1)S(1)}, bf16[80,1024]{1,0:T(8,128)(2,1)S(1)}, u32[]{:S(2)}, u32[]{:S(2)}) collective-permute-start(bf16[80,1024]{1,0:T(8,128)(2,1)S(1)} %attend.8), channel_id=1, source_target_pairs={{0,128},{8,136},{16,144},{24,152},{32,160},{40,168},{48,176},{56,1... | collective-permute-start | bytes 491528 | tf_op jit(solution)/shard_map/ppermute | solution.py:153
  54.0 17.2 %collective-permute-start.10 = (bf16[80,256]{1,0:T(8,128)(2,1)S(1)}, bf16[80,256]{1,0:T(8,128)(2,1)S(1)}, u32[]{:S(2)}, u32[]{:S(2)}) collective-permute-start(bf16[80,256]{1,0:T(8,128)(2,1)S(1)} %get-tuple-element.32), channel_id=1, source_target_pairs={{0,16},{8,24},{16,32},{24,40},{32,48},{40,56},{48,0},{56,8},{64,80... | collective-permute-start | bytes 122888 | tf_op jit(solution)/shard_map/ppermute | solution.py:153
  60.3 13.5 %collective-permute-start.11 = (bf16[80,256]{1,0:T(8,128)(2,1)S(1)}, bf16[80,256]{1,0:T(8,128)(2,1)S(1)}, u32[]{:S(2)}, u32[]{:S(2)}) collective-permute-start(bf16[80,256]{1,0:T(8,128)(2,1)S(1)} %get-tuple-element.33), channel_id=1, source_target_pairs={{0,32},{8,40},{16,48},{24,56},{32,0},{40,8},{48,16},{56,24},{64,96... | collective-permute-start | bytes 122888 | tf_op jit(solution)/shard_map/ppermute | solution.py:153
  65.8 8.1 %collective-permute-start.12 = (bf16[80,256]{1,0:T(8,128)(2,1)S(1)}, bf16[80,256]{1,0:T(8,128)(2,1)S(1)}, u32[]{:S(2)}, u32[]{:S(2)}) collective-permute-start(bf16[80,256]{1,0:T(8,128)(2,1)S(1)} %get-tuple-element.34), channel_id=1, source_target_pairs={{0,48},{8,56},{16,0},{24,8},{32,16},{40,24},{48,32},{56,40},{64,11... | collective-permute-start | bytes 122888 | tf_op jit(solution)/shard_map/ppermute | solution.py:153
  68.7 6.4 %collective-permute-start.3 = (bf16[80,256]{1,0:T(8,128)(2,1)S(1)}, bf16[80,256]{1,0:T(8,128)(2,1)S(1)}, u32[]{:S(2)}, u32[]{:S(2)}) collective-permute-start(bf16[80,256]{1,0:T(8,128)(2,1)S(1)} %get-tuple-element.24), channel_id=1, source_target_pairs={{0,16},{8,24},{16,32},{24,40},{32,48},{40,56},{48,0},{56,8},{64,80... | collective-permute-start | bytes 122888 | tf_op jit(solution)/shard_map/ppermute | solution.py:153
  69.1 8.3 %collective-permute-start.4 = (bf16[80,256]{1,0:T(8,128)(2,1)S(1)}, bf16[80,256]{1,0:T(8,128)(2,1)S(1)}, u32[]{:S(2)}, u32[]{:S(2)}) collective-permute-start(bf16[80,256]{1,0:T(8,128)(2,1)S(1)} %get-tuple-element.25), channel_id=1, source_target_pairs={{0,32},{8,40},{16,48},{24,56},{32,0},{40,8},{48,16},{56,24},{64,96... | collective-permute-start | bytes 122888 | tf_op jit(solution)/shard_map/ppermute | solution.py:153
  71.2 7.4 %collective-permute-start.5 = (bf16[80,256]{1,0:T(8,128)(2,1)S(1)}, bf16[80,256]{1,0:T(8,128)(2,1)S(1)}, u32[]{:S(2)}, u32[]{:S(2)}) collective-permute-start(bf16[80,256]{1,0:T(8,128)(2,1)S(1)} %get-tuple-element.26), channel_id=1, source_target_pairs={{0,48},{8,56},{16,0},{24,8},{32,16},{40,24},{48,32},{56,40},{64,11... | collective-permute-start | bytes 122888 | tf_op jit(solution)/shard_map/ppermute | solution.py:153
  73.9 5.2 %collective-permute-start.13 = (bf16[80,128]{1,0:T(8,128)(2,1)S(1)}, bf16[80,128]{1,0:T(8,128)(2,1)S(1)}, u32[]{:S(2)}, u32[]{:S(2)}) collective-permute-start(bf16[80,128]{1,0:T(8,128)(2,1)S(1)} %get-tuple-element.36), channel_id=1, source_target_pairs={{0,8},{8,0},{16,24},{24,16},{32,40},{40,32},{48,56},{56,48},{64,72... | collective-permute-start | bytes 61448 | tf_op jit(solution)/shard_map/ppermute | solution.py:153
  78.6 3.9 %collective-permute-start.6 = (bf16[80,128]{1,0:T(8,128)(2,1)S(1)}, bf16[80,128]{1,0:T(8,128)(2,1)S(1)}, u32[]{:S(2)}, u32[]{:S(2)}) collective-permute-start(bf16[80,128]{1,0:T(8,128)(2,1)S(1)} %get-tuple-element.28), channel_id=1, source_target_pairs={{0,8},{8,0},{16,24},{24,16},{32,40},{40,32},{48,56},{56,48},{64,72... | collective-permute-start | bytes 61448 | tf_op jit(solution)/shard_map/ppermute | solution.py:153

commit v2 on v1

v2 whole, which is shorter than its diff:
```python
import functools

import jax
import jax.numpy as jnp
from jax import lax
from jax.experimental import pallas as pl
from jax.experimental.pallas import tpu as pltpu
from jax.sharding import Mesh
from jax.sharding import PartitionSpec as P

HEAD_DIM = 64
RIM = 16
FLAT = 8
ROWS = HEAD_DIM + RIM
SCALE = 1.4426950408889634 * HEAD_DIM ** (-0.5)
Y, A, B = 4, 4, 2
TILE = 512
BF = jnp.bfloat16
F32 = jnp.float32
VMEM = pl.BlockSpec(memory_space=pltpu.VMEM)


def call(body, inputs, outs, name, scratch=(), room=16, flops=0):
    return pl.pallas_call(
        body,
        out_shape=outs,
        in_specs=[VMEM] * len(inputs),
        out_specs=jax.tree.map(lambda _: VMEM, outs),
        scratch_shapes=list(scratch),
        name=name,
        compiler_params=pltpu.CompilerParams(vmem_limit_bytes=room << 20),
        cost_estimate=pl.CostEstimate(flops=flops, transcendentals=0, bytes_accessed=1 << 18),
    )(*inputs)


def pack_body(keys, values, out):
    ranks = out.shape[0] // 2
    for j in range(ranks):
        k = keys[:, 128 * j : 128 * j + 128]
        v = values[:, 128 * j : 128 * j + 128]
        out[j] = jnp.concatenate([k[:, :HEAD_DIM], v[:, :HEAD_DIM]], axis=1)
        out[ranks + j] = jnp.concatenate([k[:, HEAD_DIM:], v[:, HEAD_DIM:]], axis=1)


def turn_body(queries, out):
    count = queries.shape[0]
    second = lax.axis_index("b") == 1
    out[HEAD_DIM:] = jnp.zeros((HEAD_DIM, count), BF)
    for i in range(0, count, TILE):
        t = queries[i : i + TILE, :].T
        out[:HEAD_DIM, i : i + TILE] = jnp.where(second, t[HEAD_DIM:], t[:HEAD_DIM])


def prep_body(pairs, out):
    t = pairs[...].T
    out[:HEAD_DIM] = t[HEAD_DIM:]
    out[HEAD_DIM:] = jnp.ones((RIM, t.shape[1]), BF)


def write_rim(lse):
    high = lse.astype(BF).astype(F32)
    rest = lse - high
    mid = rest.astype(BF).astype(F32)
    low = rest - mid
    row = lax.broadcasted_iota(jnp.int32, (RIM, lse.shape[1]), 0)
    return jnp.where(row == 0, high, jnp.where(row == 1, mid, jnp.where(row == 2, low, 0.0)))


def attend_body(shifts, queries, pairs, turned, *rest):
    outs, (even, odd) = rest[: len(shifts)], rest[len(shifts) :]
    block = outs[0].shape[1]
    y = lax.axis_index("y")
    tiles = [(b, i) for b in range(len(shifts)) for i in range(block // TILE)]

    def score(t, held):
        b, i = tiles[t]
        start = pl.multiple_of(lax.rem(y + shifts[b], Y) * block + i * TILE, TILE)
        held[...] = jnp.dot(
            pairs[...], queries[:, pl.ds(start, TILE)], preferred_element_type=F32
        )

    def gather(t, held):
        b, i = tiles[t]
        top = jnp.max(held[...], axis=0, keepdims=True) * SCALE
        weights = jnp.exp2(held[...] * SCALE - top).astype(BF)
        mixed = jnp.dot(turned[...], weights, preferred_element_type=F32)
        total = mixed[HEAD_DIM : HEAD_DIM + 1]
        span = slice(i * TILE, i * TILE + TILE)
        outs[b][:HEAD_DIM, span] = (mixed[:HEAD_DIM] / total).astype(BF)
        outs[b][HEAD_DIM:, span] = write_rim(top + jnp.log2(total)).astype(BF)

    score(0, even)
    for t in range(len(tiles)):
        here, there = (even, odd) if t % 2 == 0 else (odd, even)
        if t + 1 < len(tiles):
            score(t + 1, there)
        gather(t, here)


def attend(shifts, queries, pairs, turned, block):
    rows = pairs.shape[0]
    outs = [jax.ShapeDtypeStruct((ROWS, block), BF) for _ in shifts]
    work = len(shifts) * block * rows
    return call(
        functools.partial(attend_body, shifts),
        (queries, pairs, turned),
        outs,
        "attend",
        scratch=[pltpu.VMEM((rows, TILE), F32)] * 2,
        room=40,
        flops=work * 32,
    )


def merge(parts):
    logs = [jnp.sum(p[HEAD_DIM:].astype(F32), axis=0, keepdims=True) for p in parts]
    top = functools.reduce(jnp.maximum, logs)
    shares = [jnp.exp2(l - top) for l in logs]
    total = functools.reduce(jnp.add, shares)
    mixed = functools.reduce(
        jnp.add, [p[:HEAD_DIM].astype(F32) * s for p, s in zip(parts, shares)]
    )
    return mixed / total, top + jnp.log2(total)


def merge_body(*refs):
    ins, out = refs[:-1], refs[-1]
    width = out.shape[2]
    for i in range(out.shape[0]):
        mixed, lse = merge([r[:, i * width : i * width + width] for r in ins])
        out[i, :HEAD_DIM] = mixed
        out[i, HEAD_DIM:] = jnp.broadcast_to(lse, (FLAT, width))


def merge_flat(parts):
    logs = [p[HEAD_DIM : HEAD_DIM + 1] for p in parts]
    top = functools.reduce(jnp.maximum, logs)
    shares = [jnp.exp2(l - top) for l in logs]
    mixed = functools.reduce(jnp.add, [p[:HEAD_DIM] * s for p, s in zip(parts, shares)])
    return mixed / functools.reduce(jnp.add, shares)


def last_body(ins, out):
    heads = [merge_flat([ins[a * B + b] for a in range(A)]) for b in range(B)]
    out[...] = jnp.concatenate(heads, axis=0).T.astype(BF)


def step(part, shift):
    return lax.ppermute(part, "y", [(i, (i + shift) % Y) for i in range(Y)])


def local(queries, keys, values):
    count = queries.shape[0]
    block = count // Y
    ranks = lax.axis_size("head") * B
    tokens = keys.shape[0]
    sent = call(pack_body, (keys, values), jax.ShapeDtypeStruct((ranks, tokens, 128), BF), "pack")
    pairs = lax.all_to_all(sent, ("b", "head"), 0, 0, tiled=True).reshape(ranks * tokens, 128)
    columns = call(turn_body, (queries,), jax.ShapeDtypeStruct((128, count), BF), "turn")
    turned = call(prep_body, (pairs,), jax.ShapeDtypeStruct((ROWS, ranks * tokens), BF), "prep")
    far = attend((2,), columns, pairs, turned, block)[0]
    far = step(far, 1)
    right = attend((1,), columns, pairs, turned, block)[0]
    columns, far = lax.optimization_barrier((columns, far))
    right, far = step(right, 1), step(far, 1)
    left = attend((3,), columns, pairs, turned, block)[0]
    columns, right, far = lax.optimization_barrier((columns, right, far))
    left = step(left, 3)
    own = attend((0,), columns, pairs, turned, block)[0]
    width = block // (A * B)
    pieces = call(
        merge_body,
        (own, right, far, left),
        jax.ShapeDtypeStruct((A * B, HEAD_DIM + FLAT, width), F32),
        "merge",
    )
    pieces = lax.all_to_all(pieces, ("a", "b"), 0, 0, tiled=True)
    return call(last_body, (pieces,), jax.ShapeDtypeStruct((width, 128), BF), "last")


def solution(mesh):
    fine = Mesh(mesh.devices.reshape(Y, A, B, -1), ("y", "a", "b", "head"))
    frame = ("y", "a", "b")
    placed = (P(None, "head"), P((*frame, "head"), None), P((*frame, "head"), None))
    return jax.shard_map(
        local, mesh=fine, in_specs=placed, out_specs=P(frame, "head"), check_vma=False
    )
```

time: 84.1 us -> 76.8 us (0.913)
  starting transfers between devices: 32.9 us -> 13.3 us
  waiting for transfers between devices: 6.95 us -> 14.6 us
  blocking collectives: 13.1 us -> 19.3 us
  Pallas kernels: 28.1 us -> 27.2 us
    ppermute x14 -> x4, starting transfers between devices: 27.4 us -> 7 us  [step(): return lax.ppermute(part, 'y', [(i, (i + shift) % Y) for i in range(Y)])]
    all_to_all x1, waiting for transfers between devices: 0.01 us -> 14.6 us  [local(): lax.all_to_all(sent, ('b', 'head'), 0, 0, tiled=True)]
    ppermute x14 -> x4, waiting for transfers between devices: 6.95 us -> 0.01 us  [step(): return lax.ppermute(part, 'y', [(i, (i + shift) % Y) for i in range(Y)])]
    all_to_all x1, blocking collectives: 13.1 us -> 19.3 us  [local(): pieces = lax.all_to_all(pieces, ('a', 'b'), 0, 0, tiled=True)]
    pallas_call x17 -> x9, Pallas kernels: 28.1 us -> 27.2 us  [call(): pl.pallas_call(body, out_shape=outs, in_specs=[VMEM] * len(inputs), out_s...]
    unnamed x10 -> x6, local copies, waits for them, and re-layouts: 2.09 us -> 2.09 us
  transfers between devices with their start and end apart: 15 -> 5, of which waited for: 4 -> 1; matrix products, arithmetic and copies ran while one was open for 0% -> 0% of each run, Pallas kernels for 31% -> 24%
where the time goes in v2:
time: 76.8 us; the launch traced here: 76.5 us
  Pallas kernels  27.2 us (35%)
  blocking collectives  19.3 us (25%)
  waiting for transfers between devices  14.6 us (19%)
  starting transfers between devices  13.3 us (17%)
  local copies, waits for them, and re-layouts  2.09 us (3%)
    pallas_call x9, Pallas kernels, call(): pl.pallas_call(body, out_shape=outs, in_specs=[VMEM] * len(inputs), out_s...  27.2 us
    all_to_all x1, blocking collectives, local(): pieces = lax.all_to_all(pieces, ('a', 'b'), 0, 0, tiled=True)  19.3 us
    all_to_all x1, waiting for transfers between devices, local(): lax.all_to_all(sent, ('b', 'head'), 0, 0, tiled=True)  14.6 us
    ppermute x4, starting transfers between devices, step(): return lax.ppermute(part, 'y', [(i, (i + shift) % Y) for i in range(Y)])  7 us
    all_to_all x1, starting transfers between devices, local(): lax.all_to_all(sent, ('b', 'head'), 0, 0, tiled=True)  6.28 us
    unnamed x6, local copies, waits for them, and re-layouts  2.09 us
  transfers between devices with their start and end apart: 5, of which 1 were waited for; matrix products, arithmetic and copies ran while one was open for 0% of the time, Pallas kernels for 24%

profile of v2, /device:TPU:6, one launch (start us, length us, event | category | flops | bytes accessed | tf_op | source)
XLA Modules:
  0.0 76.5 jit_solution(16908246252369216874)
XLA Ops:
  0.0 0.0 copy-start.1
  0.0 1.0 %copy-done.1 = bf16[256,1024]{1,0:T(8,128)(2,1)S(1)} copy-done((bf16[256,1024]{1,0:T(8,128)(2,1)S(1)}, bf16[256,1024]{1,0:T(8,128)(2,1)}, u32[]{:S(2)}) %copy-start.1) | copy-done | bytes 524312
  1.0 0.0 copy-start.2
  1.0 1.0 %copy-done.2 = bf16[256,1024]{1,0:T(8,128)(2,1)S(1)} copy-done((bf16[256,1024]{1,0:T(8,128)(2,1)S(1)}, bf16[256,1024]{1,0:T(8,128)(2,1)}, u32[]{:S(2)}) %copy-start.2) | copy-done | bytes 524312
  2.1 1.3 %pack.1 = bf16[16,256,128]{2,1,0:T(8,128)(2,1)} custom-call(bf16[256,1024]{1,0:T(8,128)(2,1)S(1)} %copy-done.1, bf16[256,1024]{1,0:T(8,128)(2,1)S(1)} %copy-done.2), custom_call_target="tpu_custom_call" | custom-call | bytes 262144 | tf_op jit(solution)/shard_map/pack/pallas_call | solution.py:24
  3.4 0.0 copy-start
  3.4 6.3 %all-to-all-start = ((bf16[16,256,128]{2,1,0:T(8,128)(2,1)}), bf16[16,256,128]{2,1,0:T(8,128)(2,1)S(1)}, u32[]{:S(2)}, u32[]{:S(2)}) async-start(bf16[16,256,128]{2,1,0:T(8,128)(2,1)} %pack.1), calls=%async_computation | async-start | bytes 2097152 | tf_op jit(solution)/shard_map/all_to_all | solution.py:158
  9.7 0.0 copy-done
  9.7 0.3 turn.1.queries
  10.0 14.6 %all-to-all-done = bf16[16,256,128]{2,1,0:T(8,128)(2,1)S(1)} async-done(((bf16[16,256,128]{2,1,0:T(8,128)(2,1)}), bf16[16,256,128]{2,1,0:T(8,128)(2,1)S(1)}, u32[]{:S(2)}, u32[]{:S(2)}) %all-to-all-start) | async-done | bytes 1048608 | tf_op jit(solution)/shard_map/all_to_all | solution.py:158
  24.6 0.3 prep.1.turned
  24.9 6.1 %attend.4 = bf16[80,1024]{1,0:T(8,128)(2,1)S(1)} custom-call(bf16[128,4096]{1,0:T(8,128)(2,1)S(1)} %turn.1.queries, bf16[4096,128]{1,0:T(8,128)(2,1)S(1)} %bitcast.2, bf16[80,4096]{1,0:T(8,128)(2,1)S(1)} %prep.1.turned), custom_call_target="tpu_custom_call" | custom-call | flops 134217728 | bytes 262144 | tf_op jit(solution)/shard_map/attend/pallas_call | solution.py:24
  31.0 1.8 %collective-permute-start = (bf16[80,1024]{1,0:T(8,128)(2,1)S(1)}, bf16[80,1024]{1,0:T(8,128)(2,1)S(1)}, u32[]{:S(2)}, u32[]{:S(2)}) collective-permute-start(bf16[80,1024]{1,0:T(8,128)(2,1)S(1)} %attend.4), channel_id=1, source_target_pairs={{0,64},{64,128},{128,192},{192,0},{1,65},{65,129},{129,193},{193,1... | collective-permute-start | bytes 491528 | tf_op jit(solution)/shard_map/ppermute | solution.py:149
  32.9 6.1 %attend.5 = bf16[80,1024]{1,0:T(8,128)(2,1)S(1)} custom-call(bf16[128,4096]{1,0:T(8,128)(2,1)S(1)} %turn.1.queries, bf16[4096,128]{1,0:T(8,128)(2,1)S(1)} %bitcast.3, bf16[80,4096]{1,0:T(8,128)(2,1)S(1)} %prep.1.turned), custom_call_target="tpu_custom_call" | custom-call | flops 134217728 | bytes 262144 | tf_op jit(solution)/shard_map/attend/pallas_call | solution.py:24
  38.9 1.6 %collective-permute-start.1 = (bf16[80,1024]{1,0:T(8,128)(2,1)S(1)}, bf16[80,1024]{1,0:T(8,128)(2,1)S(1)}, u32[]{:S(2)}, u32[]{:S(2)}) collective-permute-start(bf16[80,1024]{1,0:T(8,128)(2,1)S(1)} %attend.5), channel_id=1, source_target_pairs={{0,64},{64,128},{128,192},{192,0},{1,65},{65,129},{129,193},{193,1... | collective-permute-start | bytes 491528 | tf_op jit(solution)/shard_map/ppermute | solution.py:149
  40.6 0.0 collective-permute-done
  40.6 1.3 %collective-permute-start.2 = (bf16[80,1024]{1,0:T(8,128)(2,1)S(1)}, bf16[80,1024]{1,0:T(8,128)(2,1)S(1)}, u32[]{:S(2)}, u32[]{:S(2)}) collective-permute-start(bf16[80,1024]{1,0:T(8,128)(2,1)S(1)} %collective-permute-done), channel_id=1, source_target_pairs={{0,64},{64,128},{128,192},{192,0},{1,65},{65,129},{129,193},{193,1... | collective-permute-start | bytes 491528 | tf_op jit(solution)/shard_map/ppermute | solution.py:149
  41.9 6.1 %attend.7 = bf16[80,1024]{1,0:T(8,128)(2,1)S(1)} custom-call(bf16[128,4096]{1,0:T(8,128)(2,1)S(1)} %turn.1.queries, bf16[4096,128]{1,0:T(8,128)(2,1)S(1)} %bitcast.4, bf16[80,4096]{1,0:T(8,128)(2,1)S(1)} %prep.1.turned), custom_call_target="tpu_custom_call" | custom-call | flops 134217728 | bytes 262144 | tf_op jit(solution)/shard_map/attend/pallas_call | solution.py:24
  48.0 2.2 %collective-permute-start.3 = (bf16[80,1024]{1,0:T(8,128)(2,1)S(1)}, bf16[80,1024]{1,0:T(8,128)(2,1)S(1)}, u32[]{:S(2)}, u32[]{:S(2)}) collective-permute-start(bf16[80,1024]{1,0:T(8,128)(2,1)S(1)} %attend.7), channel_id=1, source_target_pairs={{0,192},{64,0},{128,64},{192,128},{1,193},{65,1},{129,65},{193,129... | collective-permute-start | bytes 491528 | tf_op jit(solution)/shard_map/ppermute | solution.py:149
  50.2 0.0 collective-permute-done.1.refs_1_
  50.2 0.0 collective-permute-done.2.refs_2_
  50.2 6.1 %attend.6.refs_0_ = bf16[80,1024]{1,0:T(8,128)(2,1)S(1)} custom-call(bf16[128,4096]{1,0:T(8,128)(2,1)S(1)} %turn.1.queries, bf16[4096,128]{1,0:T(8,128)(2,1)S(1)} %bitcast.5, bf16[80,4096]{1,0:T(8,128)(2,1)S(1)} %prep.1.turned), custom_call_target="tpu_custom_call" | custom-call | flops 134217728 | bytes 262144 | tf_op jit(solution)/shard_map/attend/pallas_call | solution.py:24
  56.3 0.0 collective-permute-done.3.refs_3_
  56.3 0.2 merge.1
  56.5 19.3 %all_to_all.10.ins = f32[8,72,128]{2,1,0:T(8,128)S(1)} all-to-all(f32[8,72,128]{2,1,0:T(8,128)S(1)} %merge.1), channel_id=1, replica_groups=mesh['y'=4,'a'=4,'b'=2,'head'=8] {'a','b'}, dimensions={0} | all-to-all | bytes 589824 | tf_op jit(solution)/shard_map/all_to_all | solution.py:177
  75.8 0.7 last.1
Async XLA Ops:
  0.0 1.0 %copy-start.1 = (bf16[256,1024]{1,0:T(8,128)(2,1)S(1)}, bf16[256,1024]{1,0:T(8,128)(2,1)}, u32[]{:S(2)}) copy-start(bf16[256,1024]{1,0:T(8,128)(2,1)} %keys.1) | copy-start | bytes 1572868
  1.0 1.0 %copy-start.2 = (bf16[256,1024]{1,0:T(8,128)(2,1)S(1)}, bf16[256,1024]{1,0:T(8,128)(2,1)}, u32[]{:S(2)}) copy-start(bf16[256,1024]{1,0:T(8,128)(2,1)} %values.1) | copy-start | bytes 1572868
  3.4 6.3 %copy-start = (bf16[4096,128]{1,0:T(8,128)(2,1)S(1)}, bf16[4096,128]{1,0:T(8,128)(2,1)}, u32[]{:S(2)}) copy-start(bf16[4096,128]{1,0:T(8,128)(2,1)} %queries.1) | copy-start | bytes 3145732
  3.4 21.2 %all-to-all-start = ((bf16[16,256,128]{2,1,0:T(8,128)(2,1)}), bf16[16,256,128]{2,1,0:T(8,128)(2,1)S(1)}, u32[]{:S(2)}, u32[]{:S(2)}) async-start(bf16[16,256,128]{2,1,0:T(8,128)(2,1)} %pack.1), calls=%async_computation | async-start | bytes 2097152 | tf_op jit(solution)/shard_map/all_to_all | solution.py:158
  31.0 9.6 %collective-permute-start = (bf16[80,1024]{1,0:T(8,128)(2,1)S(1)}, bf16[80,1024]{1,0:T(8,128)(2,1)S(1)}, u32[]{:S(2)}, u32[]{:S(2)}) collective-permute-start(bf16[80,1024]{1,0:T(8,128)(2,1)S(1)} %attend.4), channel_id=1, source_target_pairs={{0,64},{64,128},{128,192},{192,0},{1,65},{65,129},{129,193},{193,1... | collective-permute-start | bytes 491528 | tf_op jit(solution)/shard_map/ppermute | solution.py:149
  38.9 11.3 %collective-permute-start.1 = (bf16[80,1024]{1,0:T(8,128)(2,1)S(1)}, bf16[80,1024]{1,0:T(8,128)(2,1)S(1)}, u32[]{:S(2)}, u32[]{:S(2)}) collective-permute-start(bf16[80,1024]{1,0:T(8,128)(2,1)S(1)} %attend.5), channel_id=1, source_target_pairs={{0,64},{64,128},{128,192},{192,0},{1,65},{65,129},{129,193},{193,1... | collective-permute-start | bytes 491528 | tf_op jit(solution)/shard_map/ppermute | solution.py:149
  40.6 9.6 %collective-permute-start.2 = (bf16[80,1024]{1,0:T(8,128)(2,1)S(1)}, bf16[80,1024]{1,0:T(8,128)(2,1)S(1)}, u32[]{:S(2)}, u32[]{:S(2)}) collective-permute-start(bf16[80,1024]{1,0:T(8,128)(2,1)S(1)} %collective-permute-done), channel_id=1, source_target_pairs={{0,64},{64,128},{128,192},{192,0},{1,65},{65,129},{129,193},{193,1... | collective-permute-start | bytes 491528 | tf_op jit(solution)/shard_map/ppermute | solution.py:149
  48.0 8.3 %collective-permute-start.3 = (bf16[80,1024]{1,0:T(8,128)(2,1)S(1)}, bf16[80,1024]{1,0:T(8,128)(2,1)S(1)}, u32[]{:S(2)}, u32[]{:S(2)}) collective-permute-start(bf16[80,1024]{1,0:T(8,128)(2,1)S(1)} %attend.7), channel_id=1, source_target_pairs={{0,192},{64,0},{128,64},{192,128},{1,193},{65,1},{129,65},{193,129... | collective-permute-start | bytes 491528 | tf_op jit(solution)/shard_map/ppermute | solution.py:149

commit v3 on v2

--- a/solution.py
+++ b/solution.py
@@ -15,9 +15,13 @@
 SCALE = 1.4426950408889634 * HEAD_DIM ** (-0.5)
 Y, A, B = 4, 4, 2
 TILE = 512
+RUN = 1024
+NARROW = 256
+SAFE = 60.0
 BF = jnp.bfloat16
 F32 = jnp.float32
 VMEM = pl.BlockSpec(memory_space=pltpu.VMEM)
+LENGTHS = jax.ShapeDtypeStruct((1, TILE), F32)
 
 
 def call(body, inputs, outs, name, scratch=(), room=16, flops=0):
@@ -42,19 +46,32 @@
         out[ranks + j] = jnp.concatenate([k[:, HEAD_DIM:], v[:, HEAD_DIM:]], axis=1)
 
 
-def turn_body(queries, out):
+def turn_body(queries, out, lengths):
     count = queries.shape[0]
     second = lax.axis_index("b") == 1
     out[HEAD_DIM:] = jnp.zeros((HEAD_DIM, count), BF)
+    squares = []
     for i in range(0, count, TILE):
         t = queries[i : i + TILE, :].T
-        out[:HEAD_DIM, i : i + TILE] = jnp.where(second, t[HEAD_DIM:], t[:HEAD_DIM])
-
-
-def prep_body(pairs, out):
-    t = pairs[...].T
-    out[:HEAD_DIM] = t[HEAD_DIM:]
-    out[HEAD_DIM:] = jnp.ones((RIM, t.shape[1]), BF)
+        own = jnp.where(second, t[HEAD_DIM:], t[:HEAD_DIM])
+        out[:HEAD_DIM, i : i + TILE] = own
+        squares.append(square_columns(own))
+    lengths[...] = functools.reduce(jnp.maximum, squares)
+
+
+def square_columns(columns):
+    wide = columns.astype(F32)
+    return jnp.sum(wide * wide, axis=0, keepdims=True)
+
+
+def prep_body(pairs, out, lengths):
+    squares = []
+    for i in range(0, pairs.shape[0], TILE):
+        t = pairs[i : i + TILE, :].T
+        out[:HEAD_DIM, i : i + TILE] = t[HEAD_DIM:]
+        squares.append(square_columns(t[:HEAD_DIM]))
+    out[HEAD_DIM:] = jnp.ones((RIM, pairs.shape[0]), BF)
+    lengths[...] = functools.reduce(jnp.maximum, squares)
 
 
 def write_rim(lse):
@@ -66,49 +83,54 @@
     return jnp.where(row == 0, high, jnp.where(row == 1, mid, jnp.where(row == 2, low, 0.0)))
 
 
-def attend_body(shifts, queries, pairs, turned, *rest):
-    outs, (even, odd) = rest[: len(shifts)], rest[len(shifts) :]
-    block = outs[0].shape[1]
-    y = lax.axis_index("y")
-    tiles = [(b, i) for b in range(len(shifts)) for i in range(block // TILE)]
-
-    def score(t, held):
-        b, i = tiles[t]
-        start = pl.multiple_of(lax.rem(y + shifts[b], Y) * block + i * TILE, TILE)
-        held[...] = jnp.dot(
-            pairs[...], queries[:, pl.ds(start, TILE)], preferred_element_type=F32
-        )
-
-    def gather(t, held):
-        b, i = tiles[t]
-        top = jnp.max(held[...], axis=0, keepdims=True) * SCALE
-        weights = jnp.exp2(held[...] * SCALE - top).astype(BF)
-        mixed = jnp.dot(turned[...], weights, preferred_element_type=F32)
+def attend_body(shift, queries, pairs, turned, query_lengths, key_lengths, out, held):
+    block = out.shape[1]
+    tokens = pairs.shape[0]
+    start = lax.rem(lax.axis_index("y") + shift, Y) * block
+
+    def finish(mixed, top, span):
         total = mixed[HEAD_DIM : HEAD_DIM + 1]
-        span = slice(i * TILE, i * TILE + TILE)
-        outs[b][:HEAD_DIM, span] = (mixed[:HEAD_DIM] / total).astype(BF)
-        outs[b][HEAD_DIM:, span] = write_rim(top + jnp.log2(total)).astype(BF)
-
-    score(0, even)
-    for t in range(len(tiles)):
-        here, there = (even, odd) if t % 2 == 0 else (odd, even)
-        if t + 1 < len(tiles):
-            score(t + 1, there)
-        gather(t, here)
-
-
-def attend(shifts, queries, pairs, turned, block):
-    rows = pairs.shape[0]
-    outs = [jax.ShapeDtypeStruct((ROWS, block), BF) for _ in shifts]
-    work = len(shifts) * block * rows
+        out[:HEAD_DIM, span] = (mixed[:HEAD_DIM] / total).astype(BF)
+        out[HEAD_DIM:, span] = write_rim(top + jnp.log2(total)).astype(BF)
+
+    bound = jnp.max(query_lengths[...]) * jnp.max(key_lengths[...]) * SCALE**2
+    safe = bound <= SAFE**2
+
+    @pl.when(safe)
+    def _():
+        columns = queries[:, pl.ds(pl.multiple_of(start, block), block)]
+        mixed = None
+        for r in range(0, tokens, RUN):
+            scores = jnp.dot(pairs[r : r + RUN], columns, preferred_element_type=F32)
+            weights = jnp.exp2(scores * SCALE).astype(BF)
+            more = jnp.dot(turned[:, r : r + RUN], weights, preferred_element_type=F32)
+            mixed = more if mixed is None else mixed + more
+        finish(mixed, 0.0, slice(None))
+
+    @pl.when(jnp.logical_not(safe))
+    def _():
+        @pl.loop(0, block // NARROW)
+        def _(i):
+            first = pl.multiple_of(start + i * NARROW, NARROW)
+            held[...] = jnp.dot(
+                pairs[...], queries[:, pl.ds(first, NARROW)], preferred_element_type=F32
+            )
+            top = jnp.max(held[...], axis=0, keepdims=True) * SCALE
+            weights = jnp.exp2(held[...] * SCALE - top).astype(BF)
+            mixed = jnp.dot(turned[...], weights, preferred_element_type=F32)
+            finish(mixed, top, pl.ds(pl.multiple_of(i * NARROW, NARROW), NARROW))
+
+
+def attend(shift, queries, pairs, turned, lengths, block):
+    tokens = pairs.shape[0]
     return call(
-        functools.partial(attend_body, shifts),
-        (queries, pairs, turned),
-        outs,
+        functools.partial(attend_body, shift),
+        (queries, pairs, turned, *lengths),
+        jax.ShapeDtypeStruct((ROWS, block), BF),
         "attend",
-        scratch=[pltpu.VMEM((rows, TILE), F32)] * 2,
+        scratch=[pltpu.VMEM((tokens, NARROW), F32)],
         room=40,
-        flops=work * 32,
+        flops=block * tokens * 32,
     )
 
 
@@ -156,17 +178,25 @@
     tokens = keys.shape[0]
     sent = call(pack_body, (keys, values), jax.ShapeDtypeStruct((ranks, tokens, 128), BF), "pack")
     pairs = lax.all_to_all(sent, ("b", "head"), 0, 0, tiled=True).reshape(ranks * tokens, 128)
-    columns = call(turn_body, (queries,), jax.ShapeDtypeStruct((128, count), BF), "turn")
-    turned = call(prep_body, (pairs,), jax.ShapeDtypeStruct((ROWS, ranks * tokens), BF), "prep")
-    far = attend((2,), columns, pairs, turned, block)[0]
+    columns, query_lengths = call(
+        turn_body, (queries,), (jax.ShapeDtypeStruct((128, count), BF), LENGTHS), "turn"
+    )
+    turned, key_lengths = call(
+        prep_body,
+        (pairs,),
+        (jax.ShapeDtypeStruct((ROWS, ranks * tokens), BF), LENGTHS),
+        "prep",
+    )
+    lengths = (query_lengths, key_lengths)
+    far = attend(2, columns, pairs, turned, lengths, block)
     far = step(far, 1)
-    right = attend((1,), columns, pairs, turned, block)[0]
+    right = attend(1, columns, pairs, turned, lengths, block)
     columns, far = lax.optimization_barrier((columns, far))
     right, far = step(right, 1), step(far, 1)
-    left = attend((3,), columns, pairs, turned, block)[0]
+    left = attend(3, columns, pairs, turned, lengths, block)
     columns, right, far = lax.optimization_barrier((columns, right, far))
     left = step(left, 3)
-    own = attend((0,), columns, pairs, turned, block)[0]
+    own = attend(0, columns, pairs, turned, lengths, block)
     width = block // (A * B)
     pieces = call(
         merge_body,

time: 76.8 us -> 88.7 us (1.15)
  Pallas kernels: 27.2 us -> 39.4 us
    pallas_call x9, Pallas kernels: 27.2 us -> 39.4 us  [call(): pl.pallas_call(body, out_shape=outs, in_specs=[VMEM] * len(inputs), out_s...]
  transfers between devices with their start and end apart: 5 -> 5, of which waited for: 1 -> 1; matrix products, arithmetic and copies ran while one was open for 0% -> 0% of each run, Pallas kernels for 24% -> 32%
where the time goes in v3:
time: 88.7 us; the launch traced here: 88.4 us
  Pallas kernels  39.4 us (44%)
  blocking collectives  19.3 us (22%)
  waiting for transfers between devices  14.6 us (16%)
  starting transfers between devices  12.9 us (15%)
  local copies, waits for them, and re-layouts  2.09 us (2%)
    pallas_call x9, Pallas kernels, call(): pl.pallas_call(body, out_shape=outs, in_specs=[VMEM] * len(inputs), out_s...  39.4 us
    all_to_all x1, blocking collectives, local(): pieces = lax.all_to_all(pieces, ('a', 'b'), 0, 0, tiled=True)  19.3 us
    all_to_all x1, waiting for transfers between devices, local(): lax.all_to_all(sent, ('b', 'head'), 0, 0, tiled=True)  14.6 us
    ppermute x4, starting transfers between devices, step(): return lax.ppermute(part, 'y', [(i, (i + shift) % Y) for i in range(Y)])  6.63 us
    all_to_all x1, starting transfers between devices, local(): lax.all_to_all(sent, ('b', 'head'), 0, 0, tiled=True)  6.28 us
    unnamed x6, local copies, waits for them, and re-layouts  2.09 us
  transfers between devices with their start and end apart: 5, of which 1 were waited for; matrix products, arithmetic and copies ran while one was open for 0% of the time, Pallas kernels for 32%

profile of v3, /device:TPU:6, one launch (start us, length us, event | category | flops | bytes accessed | tf_op | source)
XLA Modules:
  0.0 88.4 jit_solution(7375270336287266236)
XLA Ops:
  0.0 0.0 copy-start.1
  0.0 1.0 %copy-done.1 = bf16[256,1024]{1,0:T(8,128)(2,1)S(1)} copy-done((bf16[256,1024]{1,0:T(8,128)(2,1)S(1)}, bf16[256,1024]{1,0:T(8,128)(2,1)}, u32[]{:S(2)}) %copy-start.1) | copy-done | bytes 524312
  1.0 0.0 copy-start.2
  1.0 1.0 %copy-done.2 = bf16[256,1024]{1,0:T(8,128)(2,1)S(1)} copy-done((bf16[256,1024]{1,0:T(8,128)(2,1)S(1)}, bf16[256,1024]{1,0:T(8,128)(2,1)}, u32[]{:S(2)}) %copy-start.2) | copy-done | bytes 524312
  2.1 1.3 %pack.1 = bf16[16,256,128]{2,1,0:T(8,128)(2,1)} custom-call(bf16[256,1024]{1,0:T(8,128)(2,1)S(1)} %copy-done.1, bf16[256,1024]{1,0:T(8,128)(2,1)S(1)} %copy-done.2), custom_call_target="tpu_custom_call" | custom-call | bytes 262144 | tf_op jit(solution)/shard_map/pack/pallas_call | solution.py:28
  3.4 0.0 copy-start
  3.4 6.3 %all-to-all-start = ((bf16[16,256,128]{2,1,0:T(8,128)(2,1)}), bf16[16,256,128]{2,1,0:T(8,128)(2,1)S(1)}, u32[]{:S(2)}, u32[]{:S(2)}) async-start(bf16[16,256,128]{2,1,0:T(8,128)(2,1)} %pack.1), calls=%async_computation | async-start | bytes 2097152 | tf_op jit(solution)/shard_map/all_to_all | solution.py:180
  9.7 0.0 copy-done
  9.7 0.4 turn.1
  10.0 14.6 %all-to-all-done = bf16[16,256,128]{2,1,0:T(8,128)(2,1)S(1)} async-done(((bf16[16,256,128]{2,1,0:T(8,128)(2,1)}), bf16[16,256,128]{2,1,0:T(8,128)(2,1)S(1)}, u32[]{:S(2)}, u32[]{:S(2)}) %all-to-all-start) | async-done | bytes 1048608 | tf_op jit(solution)/shard_map/all_to_all | solution.py:180
  24.6 0.3 prep.1
  24.9 9.0 %attend.4 = bf16[80,1024]{1,0:T(8,128)(2,1)S(1)} custom-call(bf16[128,4096]{1,0:T(8,128)(2,1)S(1)} %get-tuple-element.20.queries, bf16[4096,128]{1,0:T(8,128)(2,1)S(1)} %bitcast.2, bf16[80,4096]{1,0:T(8,128)(2,1)S(1)} %get-tuple-element.15.turned, f32[1,512]{1,0:T(1,128)S(1)} %get-tuple-element.16.query_lengths, f32[1,512]{1,0:T(1,128)S(1)} %get-tuple-element.17.key_lengths), custom_call_target="tpu_custom_call" | custom-call | flops 134217728 | bytes 262144 | tf_op jit(solution)/shard_map/attend/pallas_call | solution.py:28
  34.0 1.7 %collective-permute-start = (bf16[80,1024]{1,0:T(8,128)(2,1)S(1)}, bf16[80,1024]{1,0:T(8,128)(2,1)S(1)}, u32[]{:S(2)}, u32[]{:S(2)}) collective-permute-start(bf16[80,1024]{1,0:T(8,128)(2,1)S(1)} %attend.4), channel_id=1, source_target_pairs={{0,64},{64,128},{128,192},{192,0},{1,65},{65,129},{129,193},{193,1... | collective-permute-start | bytes 491528 | tf_op jit(solution)/shard_map/ppermute | solution.py:171
  35.6 9.2 %attend.5 = bf16[80,1024]{1,0:T(8,128)(2,1)S(1)} custom-call(bf16[128,4096]{1,0:T(8,128)(2,1)S(1)} %get-tuple-element.20.queries, bf16[4096,128]{1,0:T(8,128)(2,1)S(1)} %bitcast.3, bf16[80,4096]{1,0:T(8,128)(2,1)S(1)} %get-tuple-element.15.turned, f32[1,512]{1,0:T(1,128)S(1)} %get-tuple-element.16.query_lengths, f32[1,512]{1,0:T(1,128)S(1)} %get-tuple-element.17.key_lengths), custom_call_target="tpu_custom_call" | custom-call | flops 134217728 | bytes 262144 | tf_op jit(solution)/shard_map/attend/pallas_call | solution.py:28
  44.8 1.7 %collective-permute-start.1 = (bf16[80,1024]{1,0:T(8,128)(2,1)S(1)}, bf16[80,1024]{1,0:T(8,128)(2,1)S(1)}, u32[]{:S(2)}, u32[]{:S(2)}) collective-permute-start(bf16[80,1024]{1,0:T(8,128)(2,1)S(1)} %attend.5), channel_id=1, source_target_pairs={{0,64},{64,128},{128,192},{192,0},{1,65},{65,129},{129,193},{193,1... | collective-permute-start | bytes 491528 | tf_op jit(solution)/shard_map/ppermute | solution.py:171
  46.5 0.0 collective-permute-done
  46.5 1.3 %collective-permute-start.2 = (bf16[80,1024]{1,0:T(8,128)(2,1)S(1)}, bf16[80,1024]{1,0:T(8,128)(2,1)S(1)}, u32[]{:S(2)}, u32[]{:S(2)}) collective-permute-start(bf16[80,1024]{1,0:T(8,128)(2,1)S(1)} %collective-permute-done), channel_id=1, source_target_pairs={{0,64},{64,128},{128,192},{192,0},{1,65},{65,129},{129,193},{193,1... | collective-permute-start | bytes 491528 | tf_op jit(solution)/shard_map/ppermute | solution.py:171
  47.8 9.0 %attend.7 = bf16[80,1024]{1,0:T(8,128)(2,1)S(1)} custom-call(bf16[128,4096]{1,0:T(8,128)(2,1)S(1)} %get-tuple-element.20.queries, bf16[4096,128]{1,0:T(8,128)(2,1)S(1)} %bitcast.4, bf16[80,4096]{1,0:T(8,128)(2,1)S(1)} %get-tuple-element.15.turned, f32[1,512]{1,0:T(1,128)S(1)} %get-tuple-element.16.query_lengths, f32[1,512]{1,0:T(1,128)S(1)} %get-tuple-element.17.key_lengths), custom_call_target="tpu_custom_call" | custom-call | flops 134217728 | bytes 262144 | tf_op jit(solution)/shard_map/attend/pallas_call | solution.py:28
  56.8 2.0 %collective-permute-start.3 = (bf16[80,1024]{1,0:T(8,128)(2,1)S(1)}, bf16[80,1024]{1,0:T(8,128)(2,1)S(1)}, u32[]{:S(2)}, u32[]{:S(2)}) collective-permute-start(bf16[80,1024]{1,0:T(8,128)(2,1)S(1)} %attend.7), channel_id=1, source_target_pairs={{0,192},{64,0},{128,64},{192,128},{1,193},{65,1},{129,65},{193,129... | collective-permute-start | bytes 491528 | tf_op jit(solution)/shard_map/ppermute | solution.py:171
  58.9 0.0 collective-permute-done.1.refs_1_
  58.9 0.0 collective-permute-done.2.refs_2_
  58.9 9.3 %attend.6.refs_0_ = bf16[80,1024]{1,0:T(8,128)(2,1)S(1)} custom-call(bf16[128,4096]{1,0:T(8,128)(2,1)S(1)} %get-tuple-element.20.queries, bf16[4096,128]{1,0:T(8,128)(2,1)S(1)} %bitcast.5, bf16[80,4096]{1,0:T(8,128)(2,1)S(1)} %get-tuple-element.15.turned, f32[1,512]{1,0:T(1,128)S(1)} %get-tuple-element.16.query_lengths, ...), custom_call_target="tpu_custom_call" | custom-call | flops 134217728 | bytes 262144 | tf_op jit(solution)/shard_map/attend/pallas_call | solution.py:28
  68.1 0.0 collective-permute-done.3.refs_3_
  68.1 0.2 merge.1
  68.3 19.3 %all_to_all.10.ins = f32[8,72,128]{2,1,0:T(8,128)S(1)} all-to-all(f32[8,72,128]{2,1,0:T(8,128)S(1)} %merge.1), channel_id=1, replica_groups=mesh['y'=4,'a'=4,'b'=2,'head'=8] {'a','b'}, dimensions={0} | all-to-all | bytes 589824 | tf_op jit(solution)/shard_map/all_to_all | solution.py:207
  87.6 0.7 last.1
Async XLA Ops:
  0.0 1.0 %copy-start.1 = (bf16[256,1024]{1,0:T(8,128)(2,1)S(1)}, bf16[256,1024]{1,0:T(8,128)(2,1)}, u32[]{:S(2)}) copy-start(bf16[256,1024]{1,0:T(8,128)(2,1)} %keys.1) | copy-start | bytes 1572868
  1.0 1.0 %copy-start.2 = (bf16[256,1024]{1,0:T(8,128)(2,1)S(1)}, bf16[256,1024]{1,0:T(8,128)(2,1)}, u32[]{:S(2)}) copy-start(bf16[256,1024]{1,0:T(8,128)(2,1)} %values.1) | copy-start | bytes 1572868
  3.4 6.3 %copy-start = (bf16[4096,128]{1,0:T(8,128)(2,1)S(1)}, bf16[4096,128]{1,0:T(8,128)(2,1)}, u32[]{:S(2)}) copy-start(bf16[4096,128]{1,0:T(8,128)(2,1)} %queries.1) | copy-start | bytes 3145732
  3.4 21.2 %all-to-all-start = ((bf16[16,256,128]{2,1,0:T(8,128)(2,1)}), bf16[16,256,128]{2,1,0:T(8,128)(2,1)S(1)}, u32[]{:S(2)}, u32[]{:S(2)}) async-start(bf16[16,256,128]{2,1,0:T(8,128)(2,1)} %pack.1), calls=%async_computation | async-start | bytes 2097152 | tf_op jit(solution)/shard_map/all_to_all | solution.py:180
  34.0 12.5 %collective-permute-start = (bf16[80,1024]{1,0:T(8,128)(2,1)S(1)}, bf16[80,1024]{1,0:T(8,128)(2,1)S(1)}, u32[]{:S(2)}, u32[]{:S(2)}) collective-permute-start(bf16[80,1024]{1,0:T(8,128)(2,1)S(1)} %attend.4), channel_id=1, source_target_pairs={{0,64},{64,128},{128,192},{192,0},{1,65},{65,129},{129,193},{193,1... | collective-permute-start | bytes 491528 | tf_op jit(solution)/shard_map/ppermute | solution.py:171
  44.8 14.0 %collective-permute-start.1 = (bf16[80,1024]{1,0:T(8,128)(2,1)S(1)}, bf16[80,1024]{1,0:T(8,128)(2,1)S(1)}, u32[]{:S(2)}, u32[]{:S(2)}) collective-permute-start(bf16[80,1024]{1,0:T(8,128)(2,1)S(1)} %attend.5), channel_id=1, source_target_pairs={{0,64},{64,128},{128,192},{192,0},{1,65},{65,129},{129,193},{193,1... | collective-permute-start | bytes 491528 | tf_op jit(solution)/shard_map/ppermute | solution.py:171
  46.5 12.4 %collective-permute-start.2 = (bf16[80,1024]{1,0:T(8,128)(2,1)S(1)}, bf16[80,1024]{1,0:T(8,128)(2,1)S(1)}, u32[]{:S(2)}, u32[]{:S(2)}) collective-permute-start(bf16[80,1024]{1,0:T(8,128)(2,1)S(1)} %collective-permute-done), channel_id=1, source_target_pairs={{0,64},{64,128},{128,192},{192,0},{1,65},{65,129},{129,193},{193,1... | collective-permute-start | bytes 491528 | tf_op jit(solution)/shard_map/ppermute | solution.py:171
  56.8 11.3 %collective-permute-start.3 = (bf16[80,1024]{1,0:T(8,128)(2,1)S(1)}, bf16[80,1024]{1,0:T(8,128)(2,1)S(1)}, u32[]{:S(2)}, u32[]{:S(2)}) collective-permute-start(bf16[80,1024]{1,0:T(8,128)(2,1)S(1)} %attend.7), channel_id=1, source_target_pairs={{0,192},{64,0},{128,64},{192,128},{1,193},{65,1},{129,65},{193,129... | collective-permute-start | bytes 491528 | tf_op jit(solution)/shard_map/ppermute | solution.py:171

commit v4 on v3

--- a/solution.py
+++ b/solution.py
@@ -15,6 +15,7 @@
 SCALE = 1.4426950408889634 * HEAD_DIM ** (-0.5)
 Y, A, B = 4, 4, 2
 TILE = 512
+PACKS = 2
 RUN = 1024
 NARROW = 256
 SAFE = 60.0
@@ -154,6 +155,12 @@
         out[i, HEAD_DIM:] = jnp.broadcast_to(lse, (FLAT, width))
 
 
+def join_body(mine, passing, out):
+    mixed, lse = merge([mine[...], passing[...]])
+    out[:HEAD_DIM] = mixed.astype(BF)
+    out[HEAD_DIM:] = write_rim(lse).astype(BF)
+
+
 def merge_flat(parts):
     logs = [p[HEAD_DIM : HEAD_DIM + 1] for p in parts]
     top = functools.reduce(jnp.maximum, logs)
@@ -176,7 +183,15 @@
     block = count // Y
     ranks = lax.axis_size("head") * B
     tokens = keys.shape[0]
-    sent = call(pack_body, (keys, values), jax.ShapeDtypeStruct((ranks, tokens, 128), BF), "pack")
+    part = tokens // PACKS
+    sent = pl.pallas_call(
+        pack_body,
+        grid=(PACKS,),
+        in_specs=[pl.BlockSpec((part, keys.shape[1]), lambda i: (i, 0))] * 2,
+        out_specs=pl.BlockSpec((ranks, part, 128), lambda i: (0, i, 0)),
+        out_shape=jax.ShapeDtypeStruct((ranks, tokens, 128), BF),
+        name="pack",
+    )(keys, values)
     pairs = lax.all_to_all(sent, ("b", "head"), 0, 0, tiled=True).reshape(ranks * tokens, 128)
     columns, query_lengths = call(
         turn_body, (queries,), (jax.ShapeDtypeStruct((128, count), BF), LENGTHS), "turn"
@@ -188,19 +203,19 @@
         "prep",
     )
     lengths = (query_lengths, key_lengths)
-    far = attend(2, columns, pairs, turned, lengths, block)
-    far = step(far, 1)
+    far = step(attend(2, columns, pairs, turned, lengths, block), 1)
     right = attend(1, columns, pairs, turned, lengths, block)
-    columns, far = lax.optimization_barrier((columns, far))
-    right, far = step(right, 1), step(far, 1)
+    right = call(join_body, (right, far), jax.ShapeDtypeStruct((ROWS, block), BF), "join")
+    columns, right = lax.optimization_barrier((columns, right))
     left = attend(3, columns, pairs, turned, lengths, block)
-    columns, right, far = lax.optimization_barrier((columns, right, far))
+    right = step(right, 1)
+    columns, right = lax.optimization_barrier((columns, right))
     left = step(left, 3)
     own = attend(0, columns, pairs, turned, lengths, block)
     width = block // (A * B)
     pieces = call(
         merge_body,
-        (own, right, far, left),
+        (own, right, left),
         jax.ShapeDtypeStruct((A * B, HEAD_DIM + FLAT, width), F32),
         "merge",
     )

time: 88.7 us -> 86 us (0.970)
  local copies, waits for them, and re-layouts: 2.09 us -> 0.01 us
  starting transfers between devices: 12.9 us -> 11.3 us
    pallas_call x0 -> x1, Pallas kernels: none -> 2.26 us  [local(): pl.pallas_call(pack_body, grid=(PACKS,), in_specs=[pl.BlockSpec((part, ke...]
    unnamed x6 -> x2, local copies, waits for them, and re-layouts: 2.09 us -> 0.01 us
    ppermute x4 -> x3, starting transfers between devices: 6.63 us -> 5.05 us  [step(): return lax.ppermute(part, 'y', [(i, (i + shift) % Y) for i in range(Y)])]
    pallas_call x9, Pallas kernels: 39.4 us -> 38 us  [call(): pl.pallas_call(body, out_shape=outs, in_specs=[VMEM] * len(inputs), out_s...]
  transfers between devices with their start and end apart: 5 -> 4, of which waited for: 1 -> 1; matrix products, arithmetic and copies ran while one was open for 0% -> 0% of each run, Pallas kernels for 32% -> 32%
where the time goes in v4:
time: 86 us; the launch traced here: 85.8 us
  Pallas kernels  40.2 us (47%)
  blocking collectives  19.6 us (23%)
  waiting for transfers between devices  14.6 us (17%)
  starting transfers between devices  11.3 us (13%)
    pallas_call x9, Pallas kernels, call(): pl.pallas_call(body, out_shape=outs, in_specs=[VMEM] * len(inputs), out_s...  38 us
    all_to_all x1, blocking collectives, local(): pieces = lax.all_to_all(pieces, ('a', 'b'), 0, 0, tiled=True)  19.6 us
    all_to_all x1, waiting for transfers between devices, local(): lax.all_to_all(sent, ('b', 'head'), 0, 0, tiled=True)  14.6 us
    all_to_all x1, starting transfers between devices, local(): lax.all_to_all(sent, ('b', 'head'), 0, 0, tiled=True)  6.28 us
    ppermute x3, starting transfers between devices, step(): return lax.ppermute(part, 'y', [(i, (i + shift) % Y) for i in range(Y)])  5.05 us
    pallas_call x1, Pallas kernels, local(): pl.pallas_call(pack_body, grid=(PACKS,), in_specs=[pl.BlockSpec((part, ke...  2.26 us
  transfers between devices with their start and end apart: 4, of which 1 were waited for; matrix products, arithmetic and copies ran while one was open for 0% of the time, Pallas kernels for 32%

profile of v4, /device:TPU:6, one launch (start us, length us, event | category | flops | bytes accessed | tf_op | source)
XLA Modules:
  0.0 85.8 jit_solution(7903575668941837496)
XLA Ops:
  0.0 2.3 %pack.1 = bf16[16,256,128]{2,1,0:T(8,128)(2,1)} custom-call(bf16[256,1024]{1,0:T(8,128)(2,1)} %keys.1, bf16[256,1024]{1,0:T(8,128)(2,1)} %values.1), custom_call_target="tpu_custom_call" | custom-call | tf_op jit(solution)/shard_map/pack/pallas_call | solution.py:187
  2.3 0.0 copy-start
  2.3 6.3 %all-to-all-start = ((bf16[16,256,128]{2,1,0:T(8,128)(2,1)}), bf16[16,256,128]{2,1,0:T(8,128)(2,1)S(1)}, u32[]{:S(2)}, u32[]{:S(2)}) async-start(bf16[16,256,128]{2,1,0:T(8,128)(2,1)} %pack.1), calls=%async_computation | async-start | bytes 2097152 | tf_op jit(solution)/shard_map/all_to_all | solution.py:195
  8.5 0.0 copy-done
  8.5 0.4 turn.1
  8.9 14.6 %all-to-all-done = bf16[16,256,128]{2,1,0:T(8,128)(2,1)S(1)} async-done(((bf16[16,256,128]{2,1,0:T(8,128)(2,1)}), bf16[16,256,128]{2,1,0:T(8,128)(2,1)S(1)}, u32[]{:S(2)}, u32[]{:S(2)}) %all-to-all-start) | async-done | bytes 1048608 | tf_op jit(solution)/shard_map/all_to_all | solution.py:195
  23.5 0.3 prep.1
  23.8 9.0 %attend.5 = bf16[80,1024]{1,0:T(8,128)(2,1)S(1)} custom-call(bf16[128,4096]{1,0:T(8,128)(2,1)S(1)} %get-tuple-element.19.queries, bf16[4096,128]{1,0:T(8,128)(2,1)S(1)} %bitcast.2, bf16[80,4096]{1,0:T(8,128)(2,1)S(1)} %get-tuple-element.14.turned, f32[1,512]{1,0:T(1,128)S(1)} %get-tuple-element.15.query_lengths, f32[1,512]{1,0:T(1,128)S(1)} %get-tuple-element.16.key_lengths), custom_call_target="tpu_custom_call" | custom-call | flops 134217728 | bytes 262144 | tf_op jit(solution)/shard_map/attend/pallas_call | solution.py:29
  32.8 1.7 %collective-permute-start = (bf16[80,1024]{1,0:T(8,128)(2,1)S(1)}, bf16[80,1024]{1,0:T(8,128)(2,1)S(1)}, u32[]{:S(2)}, u32[]{:S(2)}) collective-permute-start(bf16[80,1024]{1,0:T(8,128)(2,1)S(1)} %attend.5), channel_id=1, source_target_pairs={{0,64},{64,128},{128,192},{192,0},{1,65},{65,129},{129,193},{193,1... | collective-permute-start | bytes 491528 | tf_op jit(solution)/shard_map/ppermute | solution.py:178
  34.5 9.2 %attend.4.mine = bf16[80,1024]{1,0:T(8,128)(2,1)S(1)} custom-call(bf16[128,4096]{1,0:T(8,128)(2,1)S(1)} %get-tuple-element.19.queries, bf16[4096,128]{1,0:T(8,128)(2,1)S(1)} %bitcast.3, bf16[80,4096]{1,0:T(8,128)(2,1)S(1)} %get-tuple-element.14.turned, f32[1,512]{1,0:T(1,128)S(1)} %get-tuple-element.15.query_lengths, f32[1,512]{1,0:T(1,128)S(1)} %get-tuple-element.16.key_lengths), custom_call_target="tpu_custom_call" | custom-call | flops 134217728 | bytes 262144 | tf_op jit(solution)/shard_map/attend/pallas_call | solution.py:29
  43.7 0.0 collective-permute-done.passing
  43.7 0.1 join.1
  43.8 1.7 %collective-permute-start.1 = (bf16[80,1024]{1,0:T(8,128)(2,1)S(1)}, bf16[80,1024]{1,0:T(8,128)(2,1)S(1)}, u32[]{:S(2)}, u32[]{:S(2)}) collective-permute-start(bf16[80,1024]{1,0:T(8,128)(2,1)S(1)} %join.1), channel_id=1, source_target_pairs={{0,64},{64,128},{128,192},{192,0},{1,65},{65,129},{129,193},{193,1... | collective-permute-start | bytes 491528 | tf_op jit(solution)/shard_map/ppermute | solution.py:178
  45.5 9.0 %attend.7 = bf16[80,1024]{1,0:T(8,128)(2,1)S(1)} custom-call(bf16[128,4096]{1,0:T(8,128)(2,1)S(1)} %get-tuple-element.19.queries, bf16[4096,128]{1,0:T(8,128)(2,1)S(1)} %bitcast.4, bf16[80,4096]{1,0:T(8,128)(2,1)S(1)} %get-tuple-element.14.turned, f32[1,512]{1,0:T(1,128)S(1)} %get-tuple-element.15.query_lengths, f32[1,512]{1,0:T(1,128)S(1)} %get-tuple-element.16.key_lengths), custom_call_target="tpu_custom_call" | custom-call | flops 134217728 | bytes 262144 | tf_op jit(solution)/shard_map/attend/pallas_call | solution.py:29
  54.5 1.7 %collective-permute-start.2 = (bf16[80,1024]{1,0:T(8,128)(2,1)S(1)}, bf16[80,1024]{1,0:T(8,128)(2,1)S(1)}, u32[]{:S(2)}, u32[]{:S(2)}) collective-permute-start(bf16[80,1024]{1,0:T(8,128)(2,1)S(1)} %attend.7), channel_id=1, source_target_pairs={{0,192},{64,0},{128,64},{192,128},{1,193},{65,1},{129,65},{193,129... | collective-permute-start | bytes 491528 | tf_op jit(solution)/shard_map/ppermute | solution.py:178
  56.3 0.0 collective-permute-done.1.refs_1_
  56.3 9.0 %attend.6.refs_0_ = bf16[80,1024]{1,0:T(8,128)(2,1)S(1)} custom-call(bf16[128,4096]{1,0:T(8,128)(2,1)S(1)} %get-tuple-element.19.queries, bf16[4096,128]{1,0:T(8,128)(2,1)S(1)} %bitcast.5, bf16[80,4096]{1,0:T(8,128)(2,1)S(1)} %get-tuple-element.14.turned, f32[1,512]{1,0:T(1,128)S(1)} %get-tuple-element.15.query_lengths, ...), custom_call_target="tpu_custom_call" | custom-call | flops 134217728 | bytes 262144 | tf_op jit(solution)/shard_map/attend/pallas_call | solution.py:29
  65.3 0.0 collective-permute-done.2.refs_2_
  65.3 0.1 merge.1
  65.5 19.6 %all_to_all.10.ins = f32[8,72,128]{2,1,0:T(8,128)S(1)} all-to-all(f32[8,72,128]{2,1,0:T(8,128)S(1)} %merge.1), channel_id=1, replica_groups=mesh['y'=4,'a'=4,'b'=2,'head'=8] {'a','b'}, dimensions={0} | all-to-all | bytes 589824 | tf_op jit(solution)/shard_map/all_to_all | solution.py:222
  85.0 0.7 last.1
Async XLA Ops:
  2.3 6.3 %copy-start = (bf16[4096,128]{1,0:T(8,128)(2,1)S(1)}, bf16[4096,128]{1,0:T(8,128)(2,1)}, u32[]{:S(2)}) copy-start(bf16[4096,128]{1,0:T(8,128)(2,1)} %queries.1) | copy-start | bytes 3145732
  2.3 21.2 %all-to-all-start = ((bf16[16,256,128]{2,1,0:T(8,128)(2,1)}), bf16[16,256,128]{2,1,0:T(8,128)(2,1)S(1)}, u32[]{:S(2)}, u32[]{:S(2)}) async-start(bf16[16,256,128]{2,1,0:T(8,128)(2,1)} %pack.1), calls=%async_computation | async-start | bytes 2097152 | tf_op jit(solution)/shard_map/all_to_all | solution.py:195
  32.8 10.9 %collective-permute-start = (bf16[80,1024]{1,0:T(8,128)(2,1)S(1)}, bf16[80,1024]{1,0:T(8,128)(2,1)S(1)}, u32[]{:S(2)}, u32[]{:S(2)}) collective-permute-start(bf16[80,1024]{1,0:T(8,128)(2,1)S(1)} %attend.5), channel_id=1, source_target_pairs={{0,64},{64,128},{128,192},{192,0},{1,65},{65,129},{129,193},{193,1... | collective-permute-start | bytes 491528 | tf_op jit(solution)/shard_map/ppermute | solution.py:178
  43.8 12.4 %collective-permute-start.1 = (bf16[80,1024]{1,0:T(8,128)(2,1)S(1)}, bf16[80,1024]{1,0:T(8,128)(2,1)S(1)}, u32[]{:S(2)}, u32[]{:S(2)}) collective-permute-start(bf16[80,1024]{1,0:T(8,128)(2,1)S(1)} %join.1), channel_id=1, source_target_pairs={{0,64},{64,128},{128,192},{192,0},{1,65},{65,129},{129,193},{193,1... | collective-permute-start | bytes 491528 | tf_op jit(solution)/shard_map/ppermute | solution.py:178
  54.5 10.8 %collective-permute-start.2 = (bf16[80,1024]{1,0:T(8,128)(2,1)S(1)}, bf16[80,1024]{1,0:T(8,128)(2,1)S(1)}, u32[]{:S(2)}, u32[]{:S(2)}) collective-permute-start(bf16[80,1024]{1,0:T(8,128)(2,1)S(1)} %attend.7), channel_id=1, source_target_pairs={{0,192},{64,0},{128,64},{192,128},{1,193},{65,1},{129,65},{193,129... | collective-permute-start | bytes 491528 | tf_op jit(solution)/shard_map/ppermute | solution.py:178

commit v5 on v4

--- a/solution.py
+++ b/solution.py
@@ -10,7 +10,6 @@
 
 HEAD_DIM = 64
 RIM = 16
-FLAT = 8
 ROWS = HEAD_DIM + RIM
 SCALE = 1.4426950408889634 * HEAD_DIM ** (-0.5)
 Y, A, B = 4, 4, 2
@@ -151,8 +150,8 @@
     width = out.shape[2]
     for i in range(out.shape[0]):
         mixed, lse = merge([r[:, i * width : i * width + width] for r in ins])
-        out[i, :HEAD_DIM] = mixed
-        out[i, HEAD_DIM:] = jnp.broadcast_to(lse, (FLAT, width))
+        out[i, :HEAD_DIM] = mixed.astype(BF)
+        out[i, HEAD_DIM:] = write_rim(lse).astype(BF)
 
 
 def join_body(mine, passing, out):
@@ -161,16 +160,8 @@
     out[HEAD_DIM:] = write_rim(lse).astype(BF)
 
 
-def merge_flat(parts):
-    logs = [p[HEAD_DIM : HEAD_DIM + 1] for p in parts]
-    top = functools.reduce(jnp.maximum, logs)
-    shares = [jnp.exp2(l - top) for l in logs]
-    mixed = functools.reduce(jnp.add, [p[:HEAD_DIM] * s for p, s in zip(parts, shares)])
-    return mixed / functools.reduce(jnp.add, shares)
-
-
 def last_body(ins, out):
-    heads = [merge_flat([ins[a * B + b] for a in range(A)]) for b in range(B)]
+    heads = [merge([ins[a * B + b] for a in range(A)])[0] for b in range(B)]
     out[...] = jnp.concatenate(heads, axis=0).T.astype(BF)
 
 
@@ -216,7 +207,7 @@
     pieces = call(
         merge_body,
         (own, right, left),
-        jax.ShapeDtypeStruct((A * B, HEAD_DIM + FLAT, width), F32),
+        jax.ShapeDtypeStruct((A * B, ROWS, width), BF),
         "merge",
     )
     pieces = lax.all_to_all(pieces, ("a", "b"), 0, 0, tiled=True)

time: 86 us -> 83.3 us (0.969)
  blocking collectives: 19.6 us -> 16.8 us
    all_to_all x1, blocking collectives: 19.6 us -> 16.8 us  [local(): pieces = lax.all_to_all(pieces, ('a', 'b'), 0, 0, tiled=True)]
  transfers between devices with their start and end apart: 4 -> 4, of which waited for: 1 -> 1; matrix products, arithmetic and copies ran while one was open for 0% -> 0% of each run, Pallas kernels for 32% -> 33%
where the time goes in v5:
time: 83.3 us; the launch traced here: 83 us
  Pallas kernels  40.3 us (48%)
  blocking collectives  16.8 us (20%)
  waiting for transfers between devices  14.6 us (18%)
  starting transfers between devices  11.3 us (14%)
    pallas_call x9, Pallas kernels, call(): pl.pallas_call(body, out_shape=outs, in_specs=[VMEM] * len(inputs), out_s...  38 us
    all_to_all x1, blocking collectives, local(): pieces = lax.all_to_all(pieces, ('a', 'b'), 0, 0, tiled=True)  16.8 us
    all_to_all x1, waiting for transfers between devices, local(): lax.all_to_all(sent, ('b', 'head'), 0, 0, tiled=True)  14.6 us
    all_to_all x1, starting transfers between devices, local(): lax.all_to_all(sent, ('b', 'head'), 0, 0, tiled=True)  6.28 us
    ppermute x3, starting transfers between devices, step(): return lax.ppermute(part, 'y', [(i, (i + shift) % Y) for i in range(Y)])  5.05 us
    pallas_call x1, Pallas kernels, local(): pl.pallas_call(pack_body, grid=(PACKS,), in_specs=[pl.BlockSpec((part, ke...  2.26 us
  transfers between devices with their start and end apart: 4, of which 1 were waited for; matrix products, arithmetic and copies ran while one was open for 0% of the time, Pallas kernels for 33%

profile of v5, /device:TPU:6, one launch (start us, length us, event | category | flops | bytes accessed | tf_op | source)
XLA Modules:
  0.0 83.0 jit_solution(13047827172638648077)
XLA Ops:
  0.0 2.3 %pack.1 = bf16[16,256,128]{2,1,0:T(8,128)(2,1)} custom-call(bf16[256,1024]{1,0:T(8,128)(2,1)} %keys.1, bf16[256,1024]{1,0:T(8,128)(2,1)} %values.1), custom_call_target="tpu_custom_call" | custom-call | tf_op jit(solution)/shard_map/pack/pallas_call | solution.py:178
  2.3 0.0 copy-start
  2.3 6.3 %all-to-all-start = ((bf16[16,256,128]{2,1,0:T(8,128)(2,1)}), bf16[16,256,128]{2,1,0:T(8,128)(2,1)S(1)}, u32[]{:S(2)}, u32[]{:S(2)}) async-start(bf16[16,256,128]{2,1,0:T(8,128)(2,1)} %pack.1), calls=%async_computation | async-start | bytes 2097152 | tf_op jit(solution)/shard_map/all_to_all | solution.py:186
  8.5 0.0 copy-done
  8.5 0.4 turn.1
  8.9 14.6 %all-to-all-done = bf16[16,256,128]{2,1,0:T(8,128)(2,1)S(1)} async-done(((bf16[16,256,128]{2,1,0:T(8,128)(2,1)}), bf16[16,256,128]{2,1,0:T(8,128)(2,1)S(1)}, u32[]{:S(2)}, u32[]{:S(2)}) %all-to-all-start) | async-done | bytes 1048608 | tf_op jit(solution)/shard_map/all_to_all | solution.py:186
  23.5 0.3 prep.1
  23.8 9.0 %attend.5 = bf16[80,1024]{1,0:T(8,128)(2,1)S(1)} custom-call(bf16[128,4096]{1,0:T(8,128)(2,1)S(1)} %get-tuple-element.19.queries, bf16[4096,128]{1,0:T(8,128)(2,1)S(1)} %bitcast.2, bf16[80,4096]{1,0:T(8,128)(2,1)S(1)} %get-tuple-element.14.turned, f32[1,512]{1,0:T(1,128)S(1)} %get-tuple-element.15.query_lengths, f32[1,512]{1,0:T(1,128)S(1)} %get-tuple-element.16.key_lengths), custom_call_target="tpu_custom_call" | custom-call | flops 134217728 | bytes 262144 | tf_op jit(solution)/shard_map/attend/pallas_call | solution.py:28
  32.8 1.7 %collective-permute-start = (bf16[80,1024]{1,0:T(8,128)(2,1)S(1)}, bf16[80,1024]{1,0:T(8,128)(2,1)S(1)}, u32[]{:S(2)}, u32[]{:S(2)}) collective-permute-start(bf16[80,1024]{1,0:T(8,128)(2,1)S(1)} %attend.5), channel_id=1, source_target_pairs={{0,64},{64,128},{128,192},{192,0},{1,65},{65,129},{129,193},{193,1... | collective-permute-start | bytes 491528 | tf_op jit(solution)/shard_map/ppermute | solution.py:169
  34.5 9.2 %attend.4.mine = bf16[80,1024]{1,0:T(8,128)(2,1)S(1)} custom-call(bf16[128,4096]{1,0:T(8,128)(2,1)S(1)} %get-tuple-element.19.queries, bf16[4096,128]{1,0:T(8,128)(2,1)S(1)} %bitcast.3, bf16[80,4096]{1,0:T(8,128)(2,1)S(1)} %get-tuple-element.14.turned, f32[1,512]{1,0:T(1,128)S(1)} %get-tuple-element.15.query_lengths, f32[1,512]{1,0:T(1,128)S(1)} %get-tuple-element.16.key_lengths), custom_call_target="tpu_custom_call" | custom-call | flops 134217728 | bytes 262144 | tf_op jit(solution)/shard_map/attend/pallas_call | solution.py:28
  43.7 0.0 collective-permute-done.passing
  43.7 0.1 join.1
  43.8 1.7 %collective-permute-start.1 = (bf16[80,1024]{1,0:T(8,128)(2,1)S(1)}, bf16[80,1024]{1,0:T(8,128)(2,1)S(1)}, u32[]{:S(2)}, u32[]{:S(2)}) collective-permute-start(bf16[80,1024]{1,0:T(8,128)(2,1)S(1)} %join.1), channel_id=1, source_target_pairs={{0,64},{64,128},{128,192},{192,0},{1,65},{65,129},{129,193},{193,1... | collective-permute-start | bytes 491528 | tf_op jit(solution)/shard_map/ppermute | solution.py:169
  45.5 9.0 %attend.7 = bf16[80,1024]{1,0:T(8,128)(2,1)S(1)} custom-call(bf16[128,4096]{1,0:T(8,128)(2,1)S(1)} %get-tuple-element.19.queries, bf16[4096,128]{1,0:T(8,128)(2,1)S(1)} %bitcast.4, bf16[80,4096]{1,0:T(8,128)(2,1)S(1)} %get-tuple-element.14.turned, f32[1,512]{1,0:T(1,128)S(1)} %get-tuple-element.15.query_lengths, f32[1,512]{1,0:T(1,128)S(1)} %get-tuple-element.16.key_lengths), custom_call_target="tpu_custom_call" | custom-call | flops 134217728 | bytes 262144 | tf_op jit(solution)/shard_map/attend/pallas_call | solution.py:28
  54.5 1.7 %collective-permute-start.2 = (bf16[80,1024]{1,0:T(8,128)(2,1)S(1)}, bf16[80,1024]{1,0:T(8,128)(2,1)S(1)}, u32[]{:S(2)}, u32[]{:S(2)}) collective-permute-start(bf16[80,1024]{1,0:T(8,128)(2,1)S(1)} %attend.7), channel_id=1, source_target_pairs={{0,192},{64,0},{128,64},{192,128},{1,193},{65,1},{129,65},{193,129... | collective-permute-start | bytes 491528 | tf_op jit(solution)/shard_map/ppermute | solution.py:169
  56.3 0.0 collective-permute-done.1.refs_1_
  56.3 9.0 %attend.6.refs_0_ = bf16[80,1024]{1,0:T(8,128)(2,1)S(1)} custom-call(bf16[128,4096]{1,0:T(8,128)(2,1)S(1)} %get-tuple-element.19.queries, bf16[4096,128]{1,0:T(8,128)(2,1)S(1)} %bitcast.5, bf16[80,4096]{1,0:T(8,128)(2,1)S(1)} %get-tuple-element.14.turned, f32[1,512]{1,0:T(1,128)S(1)} %get-tuple-element.15.query_lengths, ...), custom_call_target="tpu_custom_call" | custom-call | flops 134217728 | bytes 262144 | tf_op jit(solution)/shard_map/attend/pallas_call | solution.py:28
  65.3 0.0 collective-permute-done.2.refs_2_
  65.3 0.2 merge.1
  65.5 16.8 %all_to_all.10.ins = bf16[8,80,128]{2,1,0:T(8,128)(2,1)S(1)} all-to-all(bf16[8,80,128]{2,1,0:T(8,128)(2,1)S(1)} %merge.1), channel_id=1, replica_groups=mesh['y'=4,'a'=4,'b'=2,'head'=8] {'a','b'}, dimensions={0} | all-to-all | bytes 327680 | tf_op jit(solution)/shard_map/all_to_all | solution.py:213
  82.3 0.7 last.1
Async XLA Ops:
  2.3 6.3 %copy-start = (bf16[4096,128]{1,0:T(8,128)(2,1)S(1)}, bf16[4096,128]{1,0:T(8,128)(2,1)}, u32[]{:S(2)}) copy-start(bf16[4096,128]{1,0:T(8,128)(2,1)} %queries.1) | copy-start | bytes 3145732
  2.3 21.2 %all-to-all-start = ((bf16[16,256,128]{2,1,0:T(8,128)(2,1)}), bf16[16,256,128]{2,1,0:T(8,128)(2,1)S(1)}, u32[]{:S(2)}, u32[]{:S(2)}) async-start(bf16[16,256,128]{2,1,0:T(8,128)(2,1)} %pack.1), calls=%async_computation | async-start | bytes 2097152 | tf_op jit(solution)/shard_map/all_to_all | solution.py:186
  32.8 10.9 %collective-permute-start = (bf16[80,1024]{1,0:T(8,128)(2,1)S(1)}, bf16[80,1024]{1,0:T(8,128)(2,1)S(1)}, u32[]{:S(2)}, u32[]{:S(2)}) collective-permute-start(bf16[80,1024]{1,0:T(8,128)(2,1)S(1)} %attend.5), channel_id=1, source_target_pairs={{0,64},{64,128},{128,192},{192,0},{1,65},{65,129},{129,193},{193,1... | collective-permute-start | bytes 491528 | tf_op jit(solution)/shard_map/ppermute | solution.py:169
  43.8 12.4 %collective-permute-start.1 = (bf16[80,1024]{1,0:T(8,128)(2,1)S(1)}, bf16[80,1024]{1,0:T(8,128)(2,1)S(1)}, u32[]{:S(2)}, u32[]{:S(2)}) collective-permute-start(bf16[80,1024]{1,0:T(8,128)(2,1)S(1)} %join.1), channel_id=1, source_target_pairs={{0,64},{64,128},{128,192},{192,0},{1,65},{65,129},{129,193},{193,1... | collective-permute-start | bytes 491528 | tf_op jit(solution)/shard_map/ppermute | solution.py:169
  54.5 10.8 %collective-permute-start.2 = (bf16[80,1024]{1,0:T(8,128)(2,1)S(1)}, bf16[80,1024]{1,0:T(8,128)(2,1)S(1)}, u32[]{:S(2)}, u32[]{:S(2)}) collective-permute-start(bf16[80,1024]{1,0:T(8,128)(2,1)S(1)} %attend.7), channel_id=1, source_target_pairs={{0,192},{64,0},{128,64},{192,128},{1,193},{65,1},{129,65},{193,129... | collective-permute-start | bytes 491528 | tf_op jit(solution)/shard_map/ppermute | solution.py:169

commit v6 on v5

--- a/solution.py
+++ b/solution.py
@@ -9,7 +9,7 @@
 from jax.sharding import PartitionSpec as P
 
 HEAD_DIM = 64
-RIM = 16
+RIM = 8
 ROWS = HEAD_DIM + RIM
 SCALE = 1.4426950408889634 * HEAD_DIM ** (-0.5)
 Y, A, B = 4, 4, 2

time: 83.3 us -> 83.2 us (level)
  no operation moved by 1% of the time
where the time goes in v6:
time: 83.2 us; the launch traced here: 82.9 us
  Pallas kernels  40.3 us (48%)
  blocking collectives  16.6 us (20%)
  waiting for transfers between devices  14.6 us (18%)
  starting transfers between devices  11.3 us (14%)
    pallas_call x9, Pallas kernels, call(): pl.pallas_call(body, out_shape=outs, in_specs=[VMEM] * len(inputs), out_s...  38 us
    all_to_all x1, blocking collectives, local(): pieces = lax.all_to_all(pieces, ('a', 'b'), 0, 0, tiled=True)  16.6 us
    all_to_all x1, waiting for transfers between devices, local(): lax.all_to_all(sent, ('b', 'head'), 0, 0, tiled=True)  14.6 us
    all_to_all x1, starting transfers between devices, local(): lax.all_to_all(sent, ('b', 'head'), 0, 0, tiled=True)  6.28 us
    ppermute x3, starting transfers between devices, step(): return lax.ppermute(part, 'y', [(i, (i + shift) % Y) for i in range(Y)])  5.04 us
    pallas_call x1, Pallas kernels, local(): pl.pallas_call(pack_body, grid=(PACKS,), in_specs=[pl.BlockSpec((part, ke...  2.26 us
  transfers between devices with their start and end apart: 4, of which 1 were waited for; matrix products, arithmetic and copies ran while one was open for 0% of the time, Pallas kernels for 33%

profile of v6, /device:TPU:6, one launch (start us, length us, event | category | flops | bytes accessed | tf_op | source)
XLA Modules:
  0.0 82.9 jit_solution(3546164104907075514)
XLA Ops:
  0.0 2.3 %pack.1 = bf16[16,256,128]{2,1,0:T(8,128)(2,1)} custom-call(bf16[256,1024]{1,0:T(8,128)(2,1)} %keys.1, bf16[256,1024]{1,0:T(8,128)(2,1)} %values.1), custom_call_target="tpu_custom_call" | custom-call | tf_op jit(solution)/shard_map/pack/pallas_call | solution.py:178
  2.3 0.0 copy-start
  2.3 6.3 %all-to-all-start = ((bf16[16,256,128]{2,1,0:T(8,128)(2,1)}), bf16[16,256,128]{2,1,0:T(8,128)(2,1)S(1)}, u32[]{:S(2)}, u32[]{:S(2)}) async-start(bf16[16,256,128]{2,1,0:T(8,128)(2,1)} %pack.1), calls=%async_computation | async-start | bytes 2097152 | tf_op jit(solution)/shard_map/all_to_all | solution.py:186
  8.5 0.0 copy-done
  8.5 0.4 turn.1
  8.9 14.6 %all-to-all-done = bf16[16,256,128]{2,1,0:T(8,128)(2,1)S(1)} async-done(((bf16[16,256,128]{2,1,0:T(8,128)(2,1)}), bf16[16,256,128]{2,1,0:T(8,128)(2,1)S(1)}, u32[]{:S(2)}, u32[]{:S(2)}) %all-to-all-start) | async-done | bytes 1048608 | tf_op jit(solution)/shard_map/all_to_all | solution.py:186
  23.5 0.3 prep.1
  23.8 9.0 %attend.5 = bf16[72,1024]{1,0:T(8,128)(2,1)S(1)} custom-call(bf16[128,4096]{1,0:T(8,128)(2,1)S(1)} %get-tuple-element.19.queries, bf16[4096,128]{1,0:T(8,128)(2,1)S(1)} %bitcast.2, bf16[72,4096]{1,0:T(8,128)(2,1)S(1)} %get-tuple-element.14.turned, f32[1,512]{1,0:T(1,128)S(1)} %get-tuple-element.15.query_lengths, f32[1,512]{1,0:T(1,128)S(1)} %get-tuple-element.16.key_lengths), custom_call_target="tpu_custom_call" | custom-call | flops 134217728 | bytes 262144 | tf_op jit(solution)/shard_map/attend/pallas_call | solution.py:28
  32.8 1.7 %collective-permute-start = (bf16[72,1024]{1,0:T(8,128)(2,1)S(1)}, bf16[72,1024]{1,0:T(8,128)(2,1)S(1)}, u32[]{:S(2)}, u32[]{:S(2)}) collective-permute-start(bf16[72,1024]{1,0:T(8,128)(2,1)S(1)} %attend.5), channel_id=1, source_target_pairs={{0,64},{64,128},{128,192},{192,0},{1,65},{65,129},{129,193},{193,1... | collective-permute-start | bytes 442376 | tf_op jit(solution)/shard_map/ppermute | solution.py:169
  34.5 9.2 %attend.4.mine = bf16[72,1024]{1,0:T(8,128)(2,1)S(1)} custom-call(bf16[128,4096]{1,0:T(8,128)(2,1)S(1)} %get-tuple-element.19.queries, bf16[4096,128]{1,0:T(8,128)(2,1)S(1)} %bitcast.3, bf16[72,4096]{1,0:T(8,128)(2,1)S(1)} %get-tuple-element.14.turned, f32[1,512]{1,0:T(1,128)S(1)} %get-tuple-element.15.query_lengths, f32[1,512]{1,0:T(1,128)S(1)} %get-tuple-element.16.key_lengths), custom_call_target="tpu_custom_call" | custom-call | flops 134217728 | bytes 262144 | tf_op jit(solution)/shard_map/attend/pallas_call | solution.py:28
  43.7 0.0 collective-permute-done.passing
  43.7 0.1 join.1
  43.8 1.7 %collective-permute-start.1 = (bf16[72,1024]{1,0:T(8,128)(2,1)S(1)}, bf16[72,1024]{1,0:T(8,128)(2,1)S(1)}, u32[]{:S(2)}, u32[]{:S(2)}) collective-permute-start(bf16[72,1024]{1,0:T(8,128)(2,1)S(1)} %join.1), channel_id=1, source_target_pairs={{0,64},{64,128},{128,192},{192,0},{1,65},{65,129},{129,193},{193,1... | collective-permute-start | bytes 442376 | tf_op jit(solution)/shard_map/ppermute | solution.py:169
  45.5 9.0 %attend.7 = bf16[72,1024]{1,0:T(8,128)(2,1)S(1)} custom-call(bf16[128,4096]{1,0:T(8,128)(2,1)S(1)} %get-tuple-element.19.queries, bf16[4096,128]{1,0:T(8,128)(2,1)S(1)} %bitcast.4, bf16[72,4096]{1,0:T(8,128)(2,1)S(1)} %get-tuple-element.14.turned, f32[1,512]{1,0:T(1,128)S(1)} %get-tuple-element.15.query_lengths, f32[1,512]{1,0:T(1,128)S(1)} %get-tuple-element.16.key_lengths), custom_call_target="tpu_custom_call" | custom-call | flops 134217728 | bytes 262144 | tf_op jit(solution)/shard_map/attend/pallas_call | solution.py:28
  54.6 1.7 %collective-permute-start.2 = (bf16[72,1024]{1,0:T(8,128)(2,1)S(1)}, bf16[72,1024]{1,0:T(8,128)(2,1)S(1)}, u32[]{:S(2)}, u32[]{:S(2)}) collective-permute-start(bf16[72,1024]{1,0:T(8,128)(2,1)S(1)} %attend.7), channel_id=1, source_target_pairs={{0,192},{64,0},{128,64},{192,128},{1,193},{65,1},{129,65},{193,129... | collective-permute-start | bytes 442376 | tf_op jit(solution)/shard_map/ppermute | solution.py:169
  56.3 0.0 collective-permute-done.1.refs_1_
  56.3 9.0 %attend.6.refs_0_ = bf16[72,1024]{1,0:T(8,128)(2,1)S(1)} custom-call(bf16[128,4096]{1,0:T(8,128)(2,1)S(1)} %get-tuple-element.19.queries, bf16[4096,128]{1,0:T(8,128)(2,1)S(1)} %bitcast.5, bf16[72,4096]{1,0:T(8,128)(2,1)S(1)} %get-tuple-element.14.turned, f32[1,512]{1,0:T(1,128)S(1)} %get-tuple-element.15.query_lengths, ...), custom_call_target="tpu_custom_call" | custom-call | flops 134217728 | bytes 262144 | tf_op jit(solution)/shard_map/attend/pallas_call | solution.py:28
  65.4 0.0 collective-permute-done.2.refs_2_
  65.4 0.2 merge.1
  65.5 16.6 %all_to_all.10.ins = bf16[8,72,128]{2,1,0:T(8,128)(2,1)S(1)} all-to-all(bf16[8,72,128]{2,1,0:T(8,128)(2,1)S(1)} %merge.1), channel_id=1, replica_groups=mesh['y'=4,'a'=4,'b'=2,'head'=8] {'a','b'}, dimensions={0} | all-to-all | bytes 294912 | tf_op jit(solution)/shard_map/all_to_all | solution.py:213
  82.1 0.7 last.1
Async XLA Ops:
  2.3 6.3 %copy-start = (bf16[4096,128]{1,0:T(8,128)(2,1)S(1)}, bf16[4096,128]{1,0:T(8,128)(2,1)}, u32[]{:S(2)}) copy-start(bf16[4096,128]{1,0:T(8,128)(2,1)} %queries.1) | copy-start | bytes 3145732
  2.3 21.2 %all-to-all-start = ((bf16[16,256,128]{2,1,0:T(8,128)(2,1)}), bf16[16,256,128]{2,1,0:T(8,128)(2,1)S(1)}, u32[]{:S(2)}, u32[]{:S(2)}) async-start(bf16[16,256,128]{2,1,0:T(8,128)(2,1)} %pack.1), calls=%async_computation | async-start | bytes 2097152 | tf_op jit(solution)/shard_map/all_to_all | solution.py:186
  32.8 10.9 %collective-permute-start = (bf16[72,1024]{1,0:T(8,128)(2,1)S(1)}, bf16[72,1024]{1,0:T(8,128)(2,1)S(1)}, u32[]{:S(2)}, u32[]{:S(2)}) collective-permute-start(bf16[72,1024]{1,0:T(8,128)(2,1)S(1)} %attend.5), channel_id=1, source_target_pairs={{0,64},{64,128},{128,192},{192,0},{1,65},{65,129},{129,193},{193,1... | collective-permute-start | bytes 442376 | tf_op jit(solution)/shard_map/ppermute | solution.py:169
  43.8 12.5 %collective-permute-start.1 = (bf16[72,1024]{1,0:T(8,128)(2,1)S(1)}, bf16[72,1024]{1,0:T(8,128)(2,1)S(1)}, u32[]{:S(2)}, u32[]{:S(2)}) collective-permute-start(bf16[72,1024]{1,0:T(8,128)(2,1)S(1)} %join.1), channel_id=1, source_target_pairs={{0,64},{64,128},{128,192},{192,0},{1,65},{65,129},{129,193},{193,1... | collective-permute-start | bytes 442376 | tf_op jit(solution)/shard_map/ppermute | solution.py:169
  54.6 10.8 %collective-permute-start.2 = (bf16[72,1024]{1,0:T(8,128)(2,1)S(1)}, bf16[72,1024]{1,0:T(8,128)(2,1)S(1)}, u32[]{:S(2)}, u32[]{:S(2)}) collective-permute-start(bf16[72,1024]{1,0:T(8,128)(2,1)S(1)} %attend.7), channel_id=1, source_target_pairs={{0,192},{64,0},{128,64},{192,128},{1,193},{65,1},{129,65},{193,129... | collective-permute-start | bytes 442376 | tf_op jit(solution)/shard_map/ppermute | solution.py:169

commit v7 on v6

--- a/solution.py
+++ b/solution.py
@@ -196,12 +196,12 @@
     lengths = (query_lengths, key_lengths)
     far = step(attend(2, columns, pairs, turned, lengths, block), 1)
     right = attend(1, columns, pairs, turned, lengths, block)
-    right = call(join_body, (right, far), jax.ShapeDtypeStruct((ROWS, block), BF), "join")
     columns, right = lax.optimization_barrier((columns, right))
     left = attend(3, columns, pairs, turned, lengths, block)
-    right = step(right, 1)
-    columns, right = lax.optimization_barrier((columns, right))
-    left = step(left, 3)
+    right, left = lax.optimization_barrier((right, left))
+    right = call(join_body, (right, far), jax.ShapeDtypeStruct((ROWS, block), BF), "join")
+    columns, right, left = lax.optimization_barrier((columns, right, left))
+    right, left = step(right, 1), step(left, 3)
     own = attend(0, columns, pairs, turned, lengths, block)
     width = block // (A * B)
     pieces = call(

time: 83.2 us -> 83.1 us (level)
  no operation moved by 1% of the time
where the time goes in v7:
time: 83.1 us; the launch traced here: 82.8 us
  Pallas kernels  40.3 us (48%)
  blocking collectives  16.6 us (20%)
  waiting for transfers between devices  14.6 us (18%)
  starting transfers between devices  11.2 us (13%)
    pallas_call x9, Pallas kernels, call(): pl.pallas_call(body, out_shape=outs, in_specs=[VMEM] * len(inputs), out_s...  38 us
    all_to_all x1, blocking collectives, local(): pieces = lax.all_to_all(pieces, ('a', 'b'), 0, 0, tiled=True)  16.6 us
    all_to_all x1, waiting for transfers between devices, local(): lax.all_to_all(sent, ('b', 'head'), 0, 0, tiled=True)  14.6 us
    all_to_all x1, starting transfers between devices, local(): lax.all_to_all(sent, ('b', 'head'), 0, 0, tiled=True)  6.28 us
    ppermute x3, starting transfers between devices, step(): return lax.ppermute(part, 'y', [(i, (i + shift) % Y) for i in range(Y)])  4.97 us
    pallas_call x1, Pallas kernels, local(): pl.pallas_call(pack_body, grid=(PACKS,), in_specs=[pl.BlockSpec((part, ke...  2.26 us
  transfers between devices with their start and end apart: 4, of which 1 were waited for; matrix products, arithmetic and copies ran while one was open for 0% of the time, Pallas kernels for 33%

profile of v7, /device:TPU:6, one launch (start us, length us, event | category | flops | bytes accessed | tf_op | source)
XLA Modules:
  0.0 82.8 jit_solution(1719566204015865766)
XLA Ops:
  0.0 2.3 %pack.1 = bf16[16,256,128]{2,1,0:T(8,128)(2,1)} custom-call(bf16[256,1024]{1,0:T(8,128)(2,1)} %keys.1, bf16[256,1024]{1,0:T(8,128)(2,1)} %values.1), custom_call_target="tpu_custom_call" | custom-call | tf_op jit(solution)/shard_map/pack/pallas_call | solution.py:178
  2.3 0.0 copy-start
  2.3 6.3 %all-to-all-start = ((bf16[16,256,128]{2,1,0:T(8,128)(2,1)}), bf16[16,256,128]{2,1,0:T(8,128)(2,1)S(1)}, u32[]{:S(2)}, u32[]{:S(2)}) async-start(bf16[16,256,128]{2,1,0:T(8,128)(2,1)} %pack.1), calls=%async_computation | async-start | bytes 2097152 | tf_op jit(solution)/shard_map/all_to_all | solution.py:186
  8.5 0.0 copy-done
  8.5 0.4 turn.1
  8.9 14.6 %all-to-all-done = bf16[16,256,128]{2,1,0:T(8,128)(2,1)S(1)} async-done(((bf16[16,256,128]{2,1,0:T(8,128)(2,1)}), bf16[16,256,128]{2,1,0:T(8,128)(2,1)S(1)}, u32[]{:S(2)}, u32[]{:S(2)}) %all-to-all-start) | async-done | bytes 1048608 | tf_op jit(solution)/shard_map/all_to_all | solution.py:186
  23.5 0.3 prep.1
  23.8 9.0 %attend.6 = bf16[72,1024]{1,0:T(8,128)(2,1)S(1)} custom-call(bf16[128,4096]{1,0:T(8,128)(2,1)S(1)} %get-tuple-element.24.queries, bf16[4096,128]{1,0:T(8,128)(2,1)S(1)} %bitcast.2, bf16[72,4096]{1,0:T(8,128)(2,1)S(1)} %get-tuple-element.17.turned, f32[1,512]{1,0:T(1,128)S(1)} %get-tuple-element.18.query_lengths, f32[1,512]{1,0:T(1,128)S(1)} %get-tuple-element.19.key_lengths), custom_call_target="tpu_custom_call" | custom-call | flops 134217728 | bytes 262144 | tf_op jit(solution)/shard_map/attend/pallas_call | solution.py:28
  32.8 1.7 %collective-permute-start = (bf16[72,1024]{1,0:T(8,128)(2,1)S(1)}, bf16[72,1024]{1,0:T(8,128)(2,1)S(1)}, u32[]{:S(2)}, u32[]{:S(2)}) collective-permute-start(bf16[72,1024]{1,0:T(8,128)(2,1)S(1)} %attend.6), channel_id=1, source_target_pairs={{0,64},{64,128},{128,192},{192,0},{1,65},{65,129},{129,193},{193,1... | collective-permute-start | bytes 442376 | tf_op jit(solution)/shard_map/ppermute | solution.py:169
  34.5 9.2 %attend.4.mine = bf16[72,1024]{1,0:T(8,128)(2,1)S(1)} custom-call(bf16[128,4096]{1,0:T(8,128)(2,1)S(1)} %get-tuple-element.24.queries, bf16[4096,128]{1,0:T(8,128)(2,1)S(1)} %bitcast.3, bf16[72,4096]{1,0:T(8,128)(2,1)S(1)} %get-tuple-element.17.turned, f32[1,512]{1,0:T(1,128)S(1)} %get-tuple-element.18.query_lengths, f32[1,512]{1,0:T(1,128)S(1)} %get-tuple-element.19.key_lengths), custom_call_target="tpu_custom_call" | custom-call | flops 134217728 | bytes 262144 | tf_op jit(solution)/shard_map/attend/pallas_call | solution.py:28
  43.7 9.0 %attend.5 = bf16[72,1024]{1,0:T(8,128)(2,1)S(1)} custom-call(bf16[128,4096]{1,0:T(8,128)(2,1)S(1)} %get-tuple-element.24.queries, bf16[4096,128]{1,0:T(8,128)(2,1)S(1)} %bitcast.4, bf16[72,4096]{1,0:T(8,128)(2,1)S(1)} %get-tuple-element.17.turned, f32[1,512]{1,0:T(1,128)S(1)} %get-tuple-element.18.query_lengths, f32[1,512]{1,0:T(1,128)S(1)} %get-tuple-element.19.key_lengths), custom_call_target="tpu_custom_call" | custom-call | flops 134217728 | bytes 262144 | tf_op jit(solution)/shard_map/attend/pallas_call | solution.py:28
  52.8 0.0 collective-permute-done.passing
  52.8 0.1 join.1
  52.9 1.7 %collective-permute-start.1 = (bf16[72,1024]{1,0:T(8,128)(2,1)S(1)}, bf16[72,1024]{1,0:T(8,128)(2,1)S(1)}, u32[]{:S(2)}, u32[]{:S(2)}) collective-permute-start(bf16[72,1024]{1,0:T(8,128)(2,1)S(1)} %join.1), channel_id=1, source_target_pairs={{0,64},{64,128},{128,192},{192,0},{1,65},{65,129},{129,193},{193,1... | collective-permute-start | bytes 442376 | tf_op jit(solution)/shard_map/ppermute | solution.py:169
  54.6 1.7 %collective-permute-start.2 = (bf16[72,1024]{1,0:T(8,128)(2,1)S(1)}, bf16[72,1024]{1,0:T(8,128)(2,1)S(1)}, u32[]{:S(2)}, u32[]{:S(2)}) collective-permute-start(bf16[72,1024]{1,0:T(8,128)(2,1)S(1)} %attend.5), channel_id=1, source_target_pairs={{0,192},{64,0},{128,64},{192,128},{1,193},{65,1},{129,65},{193,129... | collective-permute-start | bytes 442376 | tf_op jit(solution)/shard_map/ppermute | solution.py:169
  56.2 9.0 %attend.7.refs_0_ = bf16[72,1024]{1,0:T(8,128)(2,1)S(1)} custom-call(bf16[128,4096]{1,0:T(8,128)(2,1)S(1)} %get-tuple-element.24.queries, bf16[4096,128]{1,0:T(8,128)(2,1)S(1)} %bitcast.5, bf16[72,4096]{1,0:T(8,128)(2,1)S(1)} %get-tuple-element.17.turned, f32[1,512]{1,0:T(1,128)S(1)} %get-tuple-element.18.query_lengths, ...), custom_call_target="tpu_custom_call" | custom-call | flops 134217728 | bytes 262144 | tf_op jit(solution)/shard_map/attend/pallas_call | solution.py:28
  65.3 0.0 collective-permute-done.1.refs_1_
  65.3 0.0 collective-permute-done.2.refs_2_
  65.3 0.2 merge.1
  65.4 16.6 %all_to_all.10.ins = bf16[8,72,128]{2,1,0:T(8,128)(2,1)S(1)} all-to-all(bf16[8,72,128]{2,1,0:T(8,128)(2,1)S(1)} %merge.1), channel_id=1, replica_groups=mesh['y'=4,'a'=4,'b'=2,'head'=8] {'a','b'}, dimensions={0} | all-to-all | bytes 294912 | tf_op jit(solution)/shard_map/all_to_all | solution.py:213
  82.1 0.7 last.1
Async XLA Ops:
  2.3 6.3 %copy-start = (bf16[4096,128]{1,0:T(8,128)(2,1)S(1)}, bf16[4096,128]{1,0:T(8,128)(2,1)}, u32[]{:S(2)}) copy-start(bf16[4096,128]{1,0:T(8,128)(2,1)} %queries.1) | copy-start | bytes 3145732
  2.3 21.2 %all-to-all-start = ((bf16[16,256,128]{2,1,0:T(8,128)(2,1)}), bf16[16,256,128]{2,1,0:T(8,128)(2,1)S(1)}, u32[]{:S(2)}, u32[]{:S(2)}) async-start(bf16[16,256,128]{2,1,0:T(8,128)(2,1)} %pack.1), calls=%async_computation | async-start | bytes 2097152 | tf_op jit(solution)/shard_map/all_to_all | solution.py:186
  32.8 19.9 %collective-permute-start = (bf16[72,1024]{1,0:T(8,128)(2,1)S(1)}, bf16[72,1024]{1,0:T(8,128)(2,1)S(1)}, u32[]{:S(2)}, u32[]{:S(2)}) collective-permute-start(bf16[72,1024]{1,0:T(8,128)(2,1)S(1)} %attend.6), channel_id=1, source_target_pairs={{0,64},{64,128},{128,192},{192,0},{1,65},{65,129},{129,193},{193,1... | collective-permute-start | bytes 442376 | tf_op jit(solution)/shard_map/ppermute | solution.py:169
  52.9 12.4 %collective-permute-start.1 = (bf16[72,1024]{1,0:T(8,128)(2,1)S(1)}, bf16[72,1024]{1,0:T(8,128)(2,1)S(1)}, u32[]{:S(2)}, u32[]{:S(2)}) collective-permute-start(bf16[72,1024]{1,0:T(8,128)(2,1)S(1)} %join.1), channel_id=1, source_target_pairs={{0,64},{64,128},{128,192},{192,0},{1,65},{65,129},{129,193},{193,1... | collective-permute-start | bytes 442376 | tf_op jit(solution)/shard_map/ppermute | solution.py:169
  54.6 10.7 %collective-permute-start.2 = (bf16[72,1024]{1,0:T(8,128)(2,1)S(1)}, bf16[72,1024]{1,0:T(8,128)(2,1)S(1)}, u32[]{:S(2)}, u32[]{:S(2)}) collective-permute-start(bf16[72,1024]{1,0:T(8,128)(2,1)S(1)} %attend.5), channel_id=1, source_target_pairs={{0,192},{64,0},{128,64},{192,128},{1,193},{65,1},{129,65},{193,129... | collective-permute-start | bytes 442376 | tf_op jit(solution)/shard_map/ppermute | solution.py:169
